TPU v7x, 768 devices: a whole 4x8x12 slice. The times are simulated.
768 devices in a mesh: row: 32 (over y, z_hi, core), col: 24 (over x, z_lo).
Axes of the slice: x: 4, y: 8, z: 12 (z_hi: 2, z_lo: 6; z = z_hi * 6 + z_lo), core: 2. Of those that a mesh axis runs over, the one named last changes fastest.
Arguments:
- amplitudes: bfloat16 [6144, 6144], P('row', 'col'), may hold values from -6 to 6
- integrals: bfloat16 [6144, 6144], P('row', 'col'), may hold values from -0.078125 to 0.078125
- dressing: bfloat16 [6144, 3072], P(None, 'col'), may hold values from -0.078125 to 0.078125
Outputs:
- first_cycle: float32 [6144, 6144], P('row', 'col')
- second_cycle: float32 [6144, 3072], P('row', 'col')
All inputs are finite; a program needn't handle non-finite values.
Results may differ from a plain program's by a relative error of at most 0.0029.
Values may be sent and summed in bfloat16 or wider, within the bound.
No kernel may reach another device: no remote copies, remote signals or barrier semaphores. Data moves between devices by JAX's collectives and lax.ppermute only.
A program may use at most 32 MiB of HBM per device.

v0:
```python
import jax
import jax.numpy as jnp
from jax import lax
from jax.sharding import PartitionSpec as P


def per_device(amplitudes, integrals, dressing):
    amp_rows = lax.all_gather(amplitudes, "col", axis=1, tiled=True)
    first_cycle = jnp.dot(
        amp_rows,
        lax.all_gather(integrals, "row", axis=0, tiled=True),
        preferred_element_type=jnp.float32,
    )
    rounded = first_cycle.astype(jnp.bfloat16)
    row_count = rounded.shape[0]
    own_rows = lax.dynamic_slice_in_dim(dressing, lax.axis_index("row") * row_count, row_count, 0)
    wide_rows = lax.all_gather(own_rows, "col", axis=1, tiled=True)
    summed = lax.psum_scatter(
        lax.dot_general(
            rounded, wide_rows, (((0,), (0,)), ((), ())), preferred_element_type=jnp.float32
        ),
        "row",
        scatter_dimension=0,
        tiled=True,
    )
    second_cycle = lax.all_to_all(summed, "col", split_axis=1, concat_axis=0, tiled=True)
    return (first_cycle, second_cycle)


def solution(mesh):
    placed = (P("row", "col"), P("row", "col"), P(None, "col"))
    return jax.shard_map(
        per_device,
        mesh=mesh,
        in_specs=placed,
        out_specs=(P("row", "col"), P("row", "col")),
        check_vma=False,
    )
```

profile of v0, /device:TPU:16, one launch (start us, length us, event | category | flops | bytes accessed | tf_op | source)
XLA Modules:
  0.0 589.7 jit_solution(10437170095993956628)
XLA Ops:
  7.2 0.0 copy-start
  7.2 0.0 all-gather.4.cloned.1.call-start
  7.2 0.7 all-gather.4.cloned.1.call-update
  7.9 0.0 all-gather.6.cloned.1.call-start
  8.0 0.7 all-gather.6.cloned.1.call-update
  8.7 0.0 all-gather.8.cloned.1.call-start
  8.7 0.0 copy-done
  8.7 0.6 constant_dynamic-slice_fusion
  9.4 0.0 all-gather.8.cloned.1.call-update
  9.4 0.0 reduce-scatter.2.cloned.1.call-start
  9.4 146.4 %all-gather.4.cloned.1.call-done = bf16[192,6144]{1,0:T(8,128)(2,1)} async-done(((bf16[192,256]{1,0:T(8,128)(2,1)}), bf16[192,6144]{1,0:T(8,128)(2,1)}) %all-gather.4.cloned.1.call-update) | async-done | bytes 2359312 | tf_op jit(solution)/shard_map/all_gather | solution.py:8
  155.9 119.9 %all-gather.6.cloned.1.call-done = bf16[6144,256]{1,0:T(8,128)(2,1)} async-done(((bf16[192,256]{1,0:T(8,128)(2,1)}), bf16[6144,256]{1,0:T(8,128)(2,1)}) %all-gather.6.cloned.1.call-update) | async-done | bytes 3145744 | tf_op jit(solution)/shard_map/all_gather | solution.py:11
  275.7 3.4 fusion.2
  279.1 0.0 copy-start.1
  279.1 119.0 %all-gather.8.cloned.1.call-done = bf16[192,3072]{1,0:T(8,128)(2,1)} async-done(((bf16[192,128]{1,0:T(8,128)(2,1)}), bf16[192,3072]{1,0:T(8,128)(2,1)}) %all-gather.8.cloned.1.call-update) | async-done | bytes 1179664 | tf_op jit(solution)/shard_map/all_gather | solution.py:17
  398.1 3.5 fusion
  401.6 0.0 reduce-scatter.2.cloned.1.call-update
  401.6 0.0 copy-done.1
  401.6 165.0 %reduce-scatter.2.cloned.1.call-done = f32[8,3072]{1,0:T(8,128)} async-done(((f32[256,3072]{1,0:T(8,128)}), f32[8,3072]{1,0:T(8,128)}) %reduce-scatter.2.cloned.1.call-update) | async-done | bytes 98320 | tf_op jit(solution)/shard_map/reduce_scatter | solution.py:18
  566.6 16.0 %all_to_all.19 = f32[8,24,128]{2,0,1:T(8,128)S(1)} all-to-all(f32[8,24,128]{2,0,1:T(8,128)} %bitcast.8), channel_id=1, replica_groups=mesh['row'=32,'col'=24] {'col'}, dimensions={1} | all-to-all | bytes 196608 | tf_op jit(solution)/shard_map/all_to_all | solution.py:26
  582.6 0.6 copy.6
Async XLA Ops:
  7.2 1.6 copy-start
  7.2 148.7 %all-gather.4.cloned.1.call-start = ((), (), s32[]{:S(2)}) async-start(), calls=%async_computation.2 | async-start | bytes 2457600 | tf_op jit(solution)/shard_map/all_gather | solution.py:8
  7.9 267.8 %all-gather.6.cloned.1.call-start = ((), (), s32[]{:S(2)}) async-start(), calls=%async_computation.3 | async-start | bytes 3244032 | tf_op jit(solution)/shard_map/all_gather | solution.py:11
  8.7 389.4 %all-gather.8.cloned.1.call-start = ((), (), s32[]{:S(2)}) async-start(), calls=%async_computation.4 | async-start | bytes 1228800 | tf_op jit(solution)/shard_map/all_gather | solution.py:17
  9.4 557.2 %reduce-scatter.2.cloned.1.call-start = ((), (), s32[]{:S(2)}) async-start(), calls=%async_computation.5 | async-start | bytes 3244032 | tf_op jit(solution)/shard_map/reduce_scatter | solution.py:18
  279.1 122.5 %copy-start.1 = (f32[192,256]{1,0:T(8,128)}, f32[192,256]{1,0:T(8,128)S(1)}, u32[]{:S(2)}) copy-start(f32[192,256]{1,0:T(8,128)S(1)} %fusion.2) | copy-start | bytes 589828
Sparse Core Ops, SparseCore 0:
  10.3 145.5 all-gather.3
  159.8 115.9 all-gather.5
  278.6 119.4 all-gather.7
  403.3 163.2 reduce-scatter.1
where the time goes:
time: 590 us
  waiting for transfers between devices  552 us (94%)
  blocking collectives  16 us (3%)
  between operations  13.8 us (2%)
  matrix products  6.87 us (1%)
    reduce_scatter x1, waiting for transfers between devices, per_device(): lax.psum_scatter(lax.dot_general(rounded, wide_rows, (((0,), (0,)), ((),...  165 us
    all_gather x1, waiting for transfers between devices, per_device(): amp_rows = lax.all_gather(amplitudes, 'col', axis=1, tiled=True)  146 us
    all_gather x1, waiting for transfers between devices, per_device(): lax.all_gather(integrals, 'row', axis=0, tiled=True)  120 us
    all_gather x1, waiting for transfers between devices, per_device(): wide_rows = lax.all_gather(own_rows, 'col', axis=1, tiled=True)  119 us
    all_to_all x1, blocking collectives, per_device(): lax.all_to_all(summed, 'col', split_axis=1, concat_axis=0, tiled=True)  16 us
  transfers between devices with their start and end apart: 4, of which 4 were waited for; matrix products, arithmetic and copies ran while one was open for 1% of the time, Pallas kernels for 0%

commit v1 on v0

v1 whole, which is shorter than its diff:
```python
import jax
import jax.numpy as jnp
from jax import lax
from jax.experimental import pallas as pl
from jax.experimental.pallas import tpu as pltpu
from jax.sharding import Mesh, PartitionSpec as P


NY, NZH, NCO, NX, NZL = 8, 2, 2, 4, 6
ROW = ("y", "zh", "co")
COL = ("x", "zl")
OFFSETS = (0, -1, 1, -2, 2, -3, 3, 4)
F32, BF16 = jnp.float32, jnp.bfloat16
VMEM_SPEC = pl.BlockSpec(memory_space=pltpu.VMEM)


def shift(n, s):
    return [(i, (i + s) % n) for i in range(n)]


def first_kernel(a_ref, own_ref, other_ref, w_ref, wt_ref):
    y = lax.axis_index("y")
    upper = lax.axis_index("co") == 1
    total = jnp.zeros(w_ref.shape, F32)
    for step, offset in enumerate(OFFSETS):
        at = lax.rem(y + (offset + NY), NY) * 3
        rows = jnp.concatenate([a_ref[at], a_ref[at + 1], a_ref[at + 2]], axis=1)
        parts = []
        for zh in range(NZH):
            own, other = own_ref[step, zh], other_ref[step, zh]
            parts += [jnp.where(upper, other, own), jnp.where(upper, own, other)]
        total += jnp.dot(rows, jnp.concatenate(parts, axis=0), preferred_element_type=F32)
    w_ref[...] = total
    wt_ref[...] = total.T.reshape(wt_ref.shape).astype(BF16)


def second_kernel(w_ref, *refs):
    s_ref = refs[-1]
    x = lax.axis_index("x")
    for s in range(NX):
        s_ref[lax.rem(x + (NX - s), NX)] = jnp.dot(w_ref[...], refs[s][...], preferred_element_type=F32)


def permute(value, axis, n, s):
    return lax.ppermute(value, axis, shift(n, s))


def exchange(value, axis):
    return lax.all_to_all(value, axis, 0, 0, tiled=True)


def whole(amplitudes, integrals, dressing):
    rows, wide = amplitudes.shape
    deep = dressing.shape[0] // NX
    zh, x = lax.axis_index("zh"), lax.axis_index("x")

    a = exchange(jnp.broadcast_to(amplitudes[None], (NZL, rows, wide)), "zl")
    a = exchange(jnp.broadcast_to(a[None], (NX, NZL, rows, wide)), "x")
    a = a.reshape(NX * NZL, rows, wide)

    far = permute(integrals, "zh", NZH, 1)
    own = jnp.where(zh == 0, jnp.stack([integrals, far]), jnp.stack([far, integrals]))
    ahead = back = own
    held = [own]
    for _ in range(3):
        ahead = permute(ahead, "y", NY, 1)
        back = permute(back, "y", NY, -1)
        held += [ahead, back]
    last = jnp.stack([permute(ahead[0], "y", NY, 1), permute(back[1], "y", NY, -1)])
    held = jnp.stack(held + [last])
    other = permute(held, "co", NCO, 1)

    u = [lax.dynamic_slice_in_dim(dressing, x * deep, deep, 0)]
    for s in (1, 2, 3):
        piece = lax.dynamic_slice_in_dim(dressing, lax.rem(x + s, NX) * deep, deep, 0)
        u.append(permute(piece, "x", NX, s))

    first_cycle, wt = pl.pallas_call(
        first_kernel,
        out_shape=(
            jax.ShapeDtypeStruct((rows, wide), F32),
            jax.ShapeDtypeStruct((wide // 8, 8, rows), BF16),
        ),
        in_specs=[VMEM_SPEC] * 3,
        out_specs=(VMEM_SPEC,) * 2,
        name="first",
    )(a, held, other)

    wt = exchange(wt, ROW)
    wt = wt.reshape(NX, 8, 8, rows).transpose(0, 2, 1, 3).reshape(NX, 1, 8, deep)
    wt = jnp.broadcast_to(wt, (NX, NZL, 8, deep)).reshape(NX * NZL, 8, deep)
    wt = exchange(wt, COL).reshape(NX * NZL * 8, deep)

    part = pl.pallas_call(
        second_kernel,
        out_shape=jax.ShapeDtypeStruct((NX, NX * NZL * 8, dressing.shape[1]), F32),
        in_specs=[VMEM_SPEC] * 5,
        out_specs=VMEM_SPEC,
        name="second",
    )(wt, *u)
    part = exchange(part, "x")
    return first_cycle, jnp.sum(part, axis=0)


def solution(mesh):
    fine = Mesh(mesh.devices.reshape(NY, NZH, NCO, NX, NZL), ROW + COL)
    return jax.shard_map(
        whole,
        mesh=fine,
        in_specs=(P(ROW, COL), P(ROW, COL), P(None, COL)),
        out_specs=(P(ROW, COL), P(ROW, COL)),
        check_vma=False,
    )
```

time: 590 us -> 194 us (0.33)
  the two profiles are of different devices: /device:TPU:16 before, /device:TPU:1 now
where the time goes in v1:
time: 194 us; the launch traced here: 193 us
  starting transfers between devices  85.5 us (44%)
  blocking collectives  46.3 us (24%)
  waiting for transfers between devices  37.9 us (20%)
  local copies, waits for them, and re-layouts  11.9 us (6%)
  Pallas kernels  7.16 us (4%)
  other arithmetic  3.06 us (2%)
    ppermute x13, starting transfers between devices, permute(): return lax.ppermute(value, axis, shift(n, s))  61.2 us
    all_to_all x2, blocking collectives, exchange(): return lax.all_to_all(value, axis, 0, 0, tiled=True)  46.3 us
    all_to_all x3, starting transfers between devices, exchange(): return lax.all_to_all(value, axis, 0, 0, tiled=True)  24.2 us
    ppermute x13, waiting for transfers between devices, permute(): return lax.ppermute(value, axis, shift(n, s))  24 us
    all_to_all x3, waiting for transfers between devices, exchange(): return lax.all_to_all(value, axis, 0, 0, tiled=True)  13.8 us
    unnamed x20, local copies, waits for them, and re-layouts  6.56 us
    pallas_call x1, Pallas kernels, whole(): pl.pallas_call(first_kernel, out_shape=(jax.ShapeDtypeStruct((rows, wide)...  4.12 us
  transfers between devices with their start and end apart: 16, of which 7 were waited for; matrix products, arithmetic and copies ran while one was open for 5% of the time, Pallas kernels for 0%

profile of v1, /device:TPU:1, one launch (start us, length us, event | category | flops | bytes accessed | tf_op | source)
XLA Modules:
  0.0 192.7 jit_solution(11748766256727083727)
XLA Ops:
  0.6 0.0 copy-start.6
  0.6 15.8 %collective-permute-start = (bf16[192,256]{1,0:T(8,128)(2,1)}, bf16[192,256]{1,0:T(8,128)(2,1)S(1)}, u32[]{:S(2)}, u32[]{:S(2)}) collective-permute-start(bf16[192,256]{1,0:T(8,128)(2,1)} %param.4), channel_id=1, source_target_pairs={{0,48},{48,0},{1,49},{49,1},{2,50},{50,2},{3,51},{51,3},{4,52},{52... | collective-permute-start | bytes 294920 | tf_op jit(solution)/shard_map/ppermute | solution.py:45
  16.5 2.4 %collective-permute-done = bf16[192,256]{1,0:T(8,128)(2,1)S(1)} collective-permute-done((bf16[192,256]{1,0:T(8,128)(2,1)}, bf16[192,256]{1,0:T(8,128)(2,1)S(1)}, u32[]{:S(2)}, u32[]{:S(2)}) %collective-permute-start) | collective-permute-done | bytes 98336 | tf_op jit(solution)/shard_map/ppermute | solution.py:45
  18.9 1.0 maximum_select_fusion.1
  19.9 3.5 %collective-permute-start.1 = (bf16[2,192,256]{2,1,0:T(8,128)(2,1)S(1)}, bf16[2,192,256]{2,1,0:T(8,128)(2,1)S(1)}, u32[]{:S(2)}, u32[]{:S(2)}) collective-permute-start(bf16[2,192,256]{2,1,0:T(8,128)(2,1)S(1)} %maximum_select_fusion.1), channel_id=1, source_target_pairs={{0,96},{96,192},{192,288},{288,384},{384,480},{480,576},{576,672},... | collective-permute-start | bytes 589832 | tf_op jit(solution)/shard_map/ppermute | solution.py:45
  23.4 1.8 broadcast_in_dim.8
  25.1 10.8 %all-to-all-start = ((bf16[6,192,256]{2,1,0:T(8,128)(2,1)}), bf16[6,192,256]{2,1,0:T(8,128)(2,1)S(1)}, u32[]{:S(2)}, u32[]{:S(2)}) async-start(bf16[6,192,256]{2,1,0:T(8,128)(2,1)} %broadcast_in_dim.8), calls=%async_computation | async-start | bytes 1179648 | tf_op jit(solution)/shard_map/all_to_all | solution.py:49
  35.9 3.8 %collective-permute-start.2 = (bf16[2,192,256]{2,1,0:T(8,128)(2,1)S(1)}, bf16[2,192,256]{2,1,0:T(8,128)(2,1)S(1)}, u32[]{:S(2)}, u32[]{:S(2)}) collective-permute-start(bf16[2,192,256]{2,1,0:T(8,128)(2,1)S(1)} %maximum_select_fusion.1), channel_id=1, source_target_pairs={{0,672},{96,0},{192,96},{288,192},{384,288},{480,384},{576,480},{6... | collective-permute-start | bytes 589832 | tf_op jit(solution)/shard_map/ppermute | solution.py:45
  39.7 0.0 copy-done.6
  39.7 0.7 fusion
  40.4 0.0 collective-permute-done.1
  40.4 1.9 collective-permute-start.3
  42.4 0.7 bitcast_dynamic-update-slice_fusion.5
  43.1 0.0 collective-permute-done.2
  43.1 5.2 %collective-permute-start.4 = (bf16[2,192,256]{2,1,0:T(8,128)(2,1)S(1)}, bf16[2,192,256]{2,1,0:T(8,128)(2,1)S(1)}, u32[]{:S(2)}, u32[]{:S(2)}) collective-permute-start(bf16[2,192,256]{2,1,0:T(8,128)(2,1)S(1)} %collective-permute-done.2), channel_id=1, source_target_pairs={{0,672},{96,0},{192,96},{288,192},{384,288},{480,384},{576,480},{6... | collective-permute-start | bytes 589832 | tf_op jit(solution)/shard_map/ppermute | solution.py:45
  48.3 0.7 bitcast_dynamic-update-slice_fusion.4
  49.0 0.0 collective-permute-done.3
  49.0 1.9 collective-permute-start.5
  50.9 0.0 collective-permute-done.4
  50.9 5.3 %collective-permute-start.6 = (bf16[2,192,256]{2,1,0:T(8,128)(2,1)S(1)}, bf16[2,192,256]{2,1,0:T(8,128)(2,1)S(1)}, u32[]{:S(2)}, u32[]{:S(2)}) collective-permute-start(bf16[2,192,256]{2,1,0:T(8,128)(2,1)S(1)} %collective-permute-done.4), channel_id=1, source_target_pairs={{0,672},{96,0},{192,96},{288,192},{384,288},{480,384},{576,480},{6... | collective-permute-start | bytes 589832 | tf_op jit(solution)/shard_map/ppermute | solution.py:45
  56.2 0.7 bitcast_dynamic-update-slice_fusion.3
  56.9 0.7 bitcast_dynamic-update-slice_fusion.2
  57.6 1.2 collective-permute-done.6
  58.8 5.0 %collective-permute-start.8 = (bf16[192,256]{1,0:T(8,128)(2,1)S(1)}, bf16[192,256]{1,0:T(8,128)(2,1)S(1)}, u32[]{:S(2)}, u32[]{:S(2)}) collective-permute-start(bf16[192,256]{1,0:T(8,128)(2,1)S(1)} %slice_bitcast_fusion), channel_id=1, source_target_pairs={{0,672},{96,0},{192,96},{288,192},{384,288},{480,384},{576,480},{6... | collective-permute-start | bytes 294920 | tf_op jit(solution)/shard_map/ppermute | solution.py:45
  63.8 0.0 collective-permute-done.5
  63.9 1.9 collective-permute-start.7
  65.8 0.7 bitcast_dynamic-update-slice_fusion.1
  66.5 0.0 all-to-all-done
  66.5 1.7 broadcast_in_dim.9
  68.2 4.0 %all-to-all-start.1 = ((bf16[4,6,192,256]{3,2,1,0:T(8,128)(2,1)}), bf16[4,6,192,256]{3,2,1,0:T(8,128)(2,1)S(1)}, u32[]{:S(2)}, u32[]{:S(2)}) async-start(bf16[4,6,192,256]{3,2,1,0:T(8,128)(2,1)} %broadcast_in_dim.9), calls=%async_computation.1 | async-start | bytes 4718592 | tf_op jit(solution)/shard_map/all_to_all | solution.py:49
  72.2 0.7 bitcast_dynamic-update-slice_fusion
  72.9 0.0 collective-permute-done.8
  72.9 0.0 collective-permute-done.7
  72.9 0.7 fusion.1.own_ref
  73.6 6.3 %collective-permute-start.9 = (bf16[8,2,192,256]{3,2,1,0:T(8,128)(2,1)}, bf16[8,2,192,256]{3,2,1,0:T(8,128)(2,1)}, u32[]{:S(2)}, u32[]{:S(2)}) collective-permute-start(bf16[8,2,192,256]{3,2,1,0:T(8,128)(2,1)} %fusion.1.own_ref), channel_id=1, source_target_pairs={{0,24},{24,0},{1,25},{25,1},{2,26},{26,2},{3,27},{27,3},{4,28},{28... | collective-permute-start | bytes 4718600 | tf_op jit(solution)/shard_map/ppermute | solution.py:45
  79.9 3.4 %collective-permute-done.9.other_ref = bf16[8,2,192,256]{3,2,1,0:T(8,128)(2,1)} collective-permute-done((bf16[8,2,192,256]{3,2,1,0:T(8,128)(2,1)}, bf16[8,2,192,256]{3,2,1,0:T(8,128)(2,1)}, u32[]{:S(2)}, u32[]{:S(2)}) %collective-permute-start.9) | collective-permute-done | bytes 1572896 | tf_op jit(solution)/shard_map/ppermute | solution.py:45
  83.2 13.8 %all-to-all-done.1 = bf16[4,6,192,256]{3,2,1,0:T(8,128)(2,1)S(1)} async-done(((bf16[4,6,192,256]{3,2,1,0:T(8,128)(2,1)}), bf16[4,6,192,256]{3,2,1,0:T(8,128)(2,1)S(1)}, u32[]{:S(2)}, u32[]{:S(2)}) %all-to-all-start.1) | async-done | bytes 2359328 | tf_op jit(solution)/shard_map/all_to_all | solution.py:49
  97.1 0.0 copy-start
  97.1 1.4 copy-done
  98.5 4.1 %first.1 = (f32[192,256]{1,0:T(8,128)}, bf16[32,8,192]{2,1,0:T(8,128)(2,1)}) custom-call(bf16[24,192,256]{2,1,0:T(8,128)(2,1)} %bitcast.35, bf16[8,2,192,256]{3,2,1,0:T(8,128)(2,1)} %fusion.1.own_ref, bf16[8,2,192,256]{3,2,1,0:T(8,128)(2,1)} %collective-permute-done.9.other_ref), custom_call_target="tpu_custom_call" | custom-call | tf_op jit(solution)/shard_map/first/pallas_call | solution.py:78
  102.6 0.0 copy-start.2
  102.6 34.5 %all_to_all.25 = bf16[32,8,192]{2,1,0:T(8,128)(2,1)S(1)} all-to-all(bf16[32,8,192]{2,1,0:T(8,128)(2,1)} %get-tuple-element.5), channel_id=1, replica_groups=mesh['y'=8,'zh'=2,'co'=2,'x'=4,'zl'=6] {'y','zh','co'}, dimensions={0} | all-to-all | bytes 196608 | tf_op jit(solution)/shard_map/all_to_all | solution.py:49
  137.1 0.1 broadcast_in_dim.10
  137.3 0.9 broadcast_in_dim.22
  138.2 9.5 %all-to-all-start.3 = ((bf16[24,8,1536]{2,1,0:T(8,128)(2,1)}), bf16[24,8,1536]{2,1,0:T(8,128)(2,1)S(1)}, u32[]{:S(2)}, u32[]{:S(2)}) async-start(bf16[24,8,1536]{2,1,0:T(8,128)(2,1)} %bitcast.18), calls=%async_computation.3 | async-start | bytes 1179648 | tf_op jit(solution)/shard_map/all_to_all | solution.py:49
  147.7 0.0 copy-done.2
  147.7 0.9 constant_dynamic-slice_fusion
  148.5 3.2 %collective-permute-start.10 = (bf16[1536,128]{1,0:T(8,128)(2,1)S(1)}, bf16[1536,128]{1,0:T(8,128)(2,1)S(1)}, u32[]{:S(2)}, u32[]{:S(2)}) collective-permute-start(bf16[1536,128]{1,0:T(8,128)(2,1)S(1)} %get-tuple-element.7), channel_id=1, source_target_pairs={{0,6},{6,12},{12,18},{18,0},{1,7},{7,13},{13,19},{19,1},{2,8},{8,1... | collective-permute-start | bytes 1179656 | tf_op jit(solution)/shard_map/ppermute | solution.py:45
  151.7 4.3 %collective-permute-start.11 = (bf16[1536,128]{1,0:T(8,128)(2,1)S(1)}, bf16[1536,128]{1,0:T(8,128)(2,1)S(1)}, u32[]{:S(2)}, u32[]{:S(2)}) collective-permute-start(bf16[1536,128]{1,0:T(8,128)(2,1)S(1)} %get-tuple-element.9), channel_id=1, source_target_pairs={{0,12},{6,18},{12,0},{18,6},{1,13},{7,19},{13,1},{19,7},{2,14},{8,... | collective-permute-start | bytes 1179656 | tf_op jit(solution)/shard_map/ppermute | solution.py:45
  156.0 3.1 %collective-permute-start.12 = (bf16[1536,128]{1,0:T(8,128)(2,1)S(1)}, bf16[1536,128]{1,0:T(8,128)(2,1)S(1)}, u32[]{:S(2)}, u32[]{:S(2)}) collective-permute-start(bf16[1536,128]{1,0:T(8,128)(2,1)S(1)} %get-tuple-element.6), channel_id=1, source_target_pairs={{0,18},{6,0},{12,6},{18,12},{1,19},{7,1},{13,7},{19,13},{2,20},{8,... | collective-permute-start | bytes 1179656 | tf_op jit(solution)/shard_map/ppermute | solution.py:45
  159.1 5.9 %collective-permute-done.10.refs_1_ = bf16[1536,128]{1,0:T(8,128)(2,1)S(1)} collective-permute-done((bf16[1536,128]{1,0:T(8,128)(2,1)S(1)}, bf16[1536,128]{1,0:T(8,128)(2,1)S(1)}, u32[]{:S(2)}, u32[]{:S(2)}) %collective-permute-start.10) | collective-permute-done | bytes 393248 | tf_op jit(solution)/shard_map/ppermute | solution.py:45
  165.0 0.0 copy-start.3
  165.0 10.4 %collective-permute-done.11.refs_2_ = bf16[1536,128]{1,0:T(8,128)(2,1)S(1)} collective-permute-done((bf16[1536,128]{1,0:T(8,128)(2,1)S(1)}, bf16[1536,128]{1,0:T(8,128)(2,1)S(1)}, u32[]{:S(2)}, u32[]{:S(2)}) %collective-permute-start.11) | collective-permute-done | bytes 393248 | tf_op jit(solution)/shard_map/ppermute | solution.py:45
  175.4 0.0 copy-start.4
  175.4 0.8 collective-permute-done.12.refs_3_
  176.2 0.0 copy-start.5
  176.2 0.0 all-to-all-done.3
  176.2 0.0 copy-done.3
  176.2 0.0 copy-done.4
  176.2 0.7 copy-done.5
  176.9 0.2 copy-done.1
  177.2 3.0 %second.1 = f32[4,192,128]{2,1,0:T(8,128)} custom-call(bf16[192,1536]{1,0:T(8,128)(2,1)} %bitcast.36, bf16[1536,128]{1,0:T(8,128)(2,1)} %get-tuple-element.8.refs_0_, bf16[1536,128]{1,0:T(8,128)(2,1)} %copy-done.3, bf16[1536,128]{1,0:T(8,128)(2,1)} %copy-done.4, bf16[1536,128]{1,0:T(8,128)(2,1)} %copy-done.5), custom_call_target="tpu_custom_call" | custom-call | tf_op jit(solution)/shard_map/second/pallas_call | solution.py:94
  180.2 11.8 %all_to_all.26 = f32[4,192,128]{2,1,0:T(8,128)S(1)} all-to-all(f32[4,192,128]{2,1,0:T(8,128)} %second.1), channel_id=1, replica_groups=mesh['y'=8,'zh'=2,'co'=2,'x'=4,'zl'=6] {'x'}, dimensions={0} | all-to-all | bytes 786432 | tf_op jit(solution)/shard_map/all_to_all | solution.py:49
  192.0 0.7 reduce_sum.9
  (4 shorter events, 0.0 us)
Async XLA Ops:
  0.6 39.1 %copy-start.6 = (bf16[192,256]{1,0:T(8,128)(2,1)S(1)}, bf16[192,256]{1,0:T(8,128)(2,1)}, u32[]{:S(2)}) copy-start(bf16[192,256]{1,0:T(8,128)(2,1)} %param.4) | copy-start | bytes 294916
  0.6 18.2 %collective-permute-start = (bf16[192,256]{1,0:T(8,128)(2,1)}, bf16[192,256]{1,0:T(8,128)(2,1)S(1)}, u32[]{:S(2)}, u32[]{:S(2)}) collective-permute-start(bf16[192,256]{1,0:T(8,128)(2,1)} %param.4), channel_id=1, source_target_pairs={{0,48},{48,0},{1,49},{49,1},{2,50},{50,2},{3,51},{51,3},{4,52},{52... | collective-permute-start | bytes 294920 | tf_op jit(solution)/shard_map/ppermute | solution.py:45
  19.9 20.6 %collective-permute-start.1 = (bf16[2,192,256]{2,1,0:T(8,128)(2,1)S(1)}, bf16[2,192,256]{2,1,0:T(8,128)(2,1)S(1)}, u32[]{:S(2)}, u32[]{:S(2)}) collective-permute-start(bf16[2,192,256]{2,1,0:T(8,128)(2,1)S(1)} %maximum_select_fusion.1), channel_id=1, source_target_pairs={{0,96},{96,192},{192,288},{288,384},{384,480},{480,576},{576,672},... | collective-permute-start | bytes 589832 | tf_op jit(solution)/shard_map/ppermute | solution.py:45
  25.1 41.4 %all-to-all-start = ((bf16[6,192,256]{2,1,0:T(8,128)(2,1)}), bf16[6,192,256]{2,1,0:T(8,128)(2,1)S(1)}, u32[]{:S(2)}, u32[]{:S(2)}) async-start(bf16[6,192,256]{2,1,0:T(8,128)(2,1)} %broadcast_in_dim.8), calls=%async_computation | async-start | bytes 1179648 | tf_op jit(solution)/shard_map/all_to_all | solution.py:49
  35.9 7.2 %collective-permute-start.2 = (bf16[2,192,256]{2,1,0:T(8,128)(2,1)S(1)}, bf16[2,192,256]{2,1,0:T(8,128)(2,1)S(1)}, u32[]{:S(2)}, u32[]{:S(2)}) collective-permute-start(bf16[2,192,256]{2,1,0:T(8,128)(2,1)S(1)} %maximum_select_fusion.1), channel_id=1, source_target_pairs={{0,672},{96,0},{192,96},{288,192},{384,288},{480,384},{576,480},{6... | collective-permute-start | bytes 589832 | tf_op jit(solution)/shard_map/ppermute | solution.py:45
  40.4 8.5 %collective-permute-start.3 = (bf16[2,192,256]{2,1,0:T(8,128)(2,1)S(1)}, bf16[2,192,256]{2,1,0:T(8,128)(2,1)S(1)}, u32[]{:S(2)}, u32[]{:S(2)}) collective-permute-start(bf16[2,192,256]{2,1,0:T(8,128)(2,1)S(1)} %collective-permute-done.1), channel_id=1, source_target_pairs={{0,96},{96,192},{192,288},{288,384},{384,480},{480,576},{576,672},... | collective-permute-start | bytes 589832 | tf_op jit(solution)/shard_map/ppermute | solution.py:45
  43.1 7.8 %collective-permute-start.4 = (bf16[2,192,256]{2,1,0:T(8,128)(2,1)S(1)}, bf16[2,192,256]{2,1,0:T(8,128)(2,1)S(1)}, u32[]{:S(2)}, u32[]{:S(2)}) collective-permute-start(bf16[2,192,256]{2,1,0:T(8,128)(2,1)S(1)} %collective-permute-done.2), channel_id=1, source_target_pairs={{0,672},{96,0},{192,96},{288,192},{384,288},{480,384},{576,480},{6... | collective-permute-start | bytes 589832 | tf_op jit(solution)/shard_map/ppermute | solution.py:45
  49.0 14.9 %collective-permute-start.5 = (bf16[2,192,256]{2,1,0:T(8,128)(2,1)S(1)}, bf16[2,192,256]{2,1,0:T(8,128)(2,1)S(1)}, u32[]{:S(2)}, u32[]{:S(2)}) collective-permute-start(bf16[2,192,256]{2,1,0:T(8,128)(2,1)S(1)} %collective-permute-done.3), channel_id=1, source_target_pairs={{0,96},{96,192},{192,288},{288,384},{384,480},{480,576},{576,672},... | collective-permute-start | bytes 589832 | tf_op jit(solution)/shard_map/ppermute | solution.py:45
  50.9 7.9 %collective-permute-start.6 = (bf16[2,192,256]{2,1,0:T(8,128)(2,1)S(1)}, bf16[2,192,256]{2,1,0:T(8,128)(2,1)S(1)}, u32[]{:S(2)}, u32[]{:S(2)}) collective-permute-start(bf16[2,192,256]{2,1,0:T(8,128)(2,1)S(1)} %collective-permute-done.4), channel_id=1, source_target_pairs={{0,672},{96,0},{192,96},{288,192},{384,288},{480,384},{576,480},{6... | collective-permute-start | bytes 589832 | tf_op jit(solution)/shard_map/ppermute | solution.py:45
  58.8 14.1 %collective-permute-start.8 = (bf16[192,256]{1,0:T(8,128)(2,1)S(1)}, bf16[192,256]{1,0:T(8,128)(2,1)S(1)}, u32[]{:S(2)}, u32[]{:S(2)}) collective-permute-start(bf16[192,256]{1,0:T(8,128)(2,1)S(1)} %slice_bitcast_fusion), channel_id=1, source_target_pairs={{0,672},{96,0},{192,96},{288,192},{384,288},{480,384},{576,480},{6... | collective-permute-start | bytes 294920 | tf_op jit(solution)/shard_map/ppermute | solution.py:45
  63.9 9.0 %collective-permute-start.7 = (bf16[192,256]{1,0:T(8,128)(2,1)S(1)}, bf16[192,256]{1,0:T(8,128)(2,1)S(1)}, u32[]{:S(2)}, u32[]{:S(2)}) collective-permute-start(bf16[192,256]{1,0:T(8,128)(2,1)S(1)} %slice_bitcast_fusion.1), channel_id=1, source_target_pairs={{0,96},{96,192},{192,288},{288,384},{384,480},{480,576},{576,672},... | collective-permute-start | bytes 294920 | tf_op jit(solution)/shard_map/ppermute | solution.py:45
  68.2 28.9 %all-to-all-start.1 = ((bf16[4,6,192,256]{3,2,1,0:T(8,128)(2,1)}), bf16[4,6,192,256]{3,2,1,0:T(8,128)(2,1)S(1)}, u32[]{:S(2)}, u32[]{:S(2)}) async-start(bf16[4,6,192,256]{3,2,1,0:T(8,128)(2,1)} %broadcast_in_dim.9), calls=%async_computation.1 | async-start | bytes 4718592 | tf_op jit(solution)/shard_map/all_to_all | solution.py:49
  73.6 9.6 %collective-permute-start.9 = (bf16[8,2,192,256]{3,2,1,0:T(8,128)(2,1)}, bf16[8,2,192,256]{3,2,1,0:T(8,128)(2,1)}, u32[]{:S(2)}, u32[]{:S(2)}) collective-permute-start(bf16[8,2,192,256]{3,2,1,0:T(8,128)(2,1)} %fusion.1.own_ref), channel_id=1, source_target_pairs={{0,24},{24,0},{1,25},{25,1},{2,26},{26,2},{3,27},{27,3},{4,28},{28... | collective-permute-start | bytes 4718600 | tf_op jit(solution)/shard_map/ppermute | solution.py:45
  97.1 1.4 copy-start
  102.6 45.0 %copy-start.2 = (bf16[6144,128]{1,0:T(8,128)(2,1)S(1)}, bf16[6144,128]{1,0:T(8,128)(2,1)}, u32[]{:S(2)}) copy-start(bf16[6144,128]{1,0:T(8,128)(2,1)} %param.5) | copy-start | bytes 4718596
  138.2 38.1 %all-to-all-start.3 = ((bf16[24,8,1536]{2,1,0:T(8,128)(2,1)}), bf16[24,8,1536]{2,1,0:T(8,128)(2,1)S(1)}, u32[]{:S(2)}, u32[]{:S(2)}) async-start(bf16[24,8,1536]{2,1,0:T(8,128)(2,1)} %bitcast.18), calls=%async_computation.3 | async-start | bytes 1179648 | tf_op jit(solution)/shard_map/all_to_all | solution.py:49
  148.5 16.5 %collective-permute-start.10 = (bf16[1536,128]{1,0:T(8,128)(2,1)S(1)}, bf16[1536,128]{1,0:T(8,128)(2,1)S(1)}, u32[]{:S(2)}, u32[]{:S(2)}) collective-permute-start(bf16[1536,128]{1,0:T(8,128)(2,1)S(1)} %get-tuple-element.7), channel_id=1, source_target_pairs={{0,6},{6,12},{12,18},{18,0},{1,7},{7,13},{13,19},{19,1},{2,8},{8,1... | collective-permute-start | bytes 1179656 | tf_op jit(solution)/shard_map/ppermute | solution.py:45
  151.7 23.7 %collective-permute-start.11 = (bf16[1536,128]{1,0:T(8,128)(2,1)S(1)}, bf16[1536,128]{1,0:T(8,128)(2,1)S(1)}, u32[]{:S(2)}, u32[]{:S(2)}) collective-permute-start(bf16[1536,128]{1,0:T(8,128)(2,1)S(1)} %get-tuple-element.9), channel_id=1, source_target_pairs={{0,12},{6,18},{12,0},{18,6},{1,13},{7,19},{13,1},{19,7},{2,14},{8,... | collective-permute-start | bytes 1179656 | tf_op jit(solution)/shard_map/ppermute | solution.py:45
  156.0 20.2 %collective-permute-start.12 = (bf16[1536,128]{1,0:T(8,128)(2,1)S(1)}, bf16[1536,128]{1,0:T(8,128)(2,1)S(1)}, u32[]{:S(2)}, u32[]{:S(2)}) collective-permute-start(bf16[1536,128]{1,0:T(8,128)(2,1)S(1)} %get-tuple-element.6), channel_id=1, source_target_pairs={{0,18},{6,0},{12,6},{18,12},{1,19},{7,1},{13,7},{19,13},{2,20},{8,... | collective-permute-start | bytes 1179656 | tf_op jit(solution)/shard_map/ppermute | solution.py:45
  165.0 11.2 %copy-start.3 = (bf16[1536,128]{1,0:T(8,128)(2,1)}, bf16[1536,128]{1,0:T(8,128)(2,1)S(1)}, u32[]{:S(2)}) copy-start(bf16[1536,128]{1,0:T(8,128)(2,1)S(1)} %collective-permute-done.10.refs_1_) | copy-start | bytes 1179652
  175.4 0.8 copy-start.4
  176.2 0.7 copy-start.5
  176.2 1.0 copy-start.1

commit v2 on v1

v2 whole, which is shorter than its diff:
```python
import jax
import jax.numpy as jnp
from jax import lax
from jax.experimental import pallas as pl
from jax.experimental.pallas import tpu as pltpu
from jax.sharding import Mesh, PartitionSpec as P


NY, NZH, NCO, NX, NZL = 8, 2, 2, 4, 6
ROW = ("y", "zh", "co")
COL = ("x", "zl")
F32, BF16 = jnp.float32, jnp.bfloat16
VMEM_SPEC = pl.BlockSpec(memory_space=pltpu.VMEM)


def shift(n, s):
    return [(i, (i + s) % n) for i in range(n)]


def permute(value, axis, n, s):
    return lax.ppermute(value, axis, shift(n, s))


def opposed(value, s):
    pairs = [
        (y * NCO + co, (y + (1 - 2 * co) * s) % NY * NCO + co) for y in range(NY) for co in range(NCO)
    ]
    return lax.ppermute(value, ("y", "co"), pairs)


def exchange(value, axis):
    return lax.all_to_all(value, axis, 0, 0, tiled=True)


def first_kernel(*refs):
    a_refs, v_refs, (w_ref, wt_ref, a_all, sems) = refs[:5], refs[5:14], refs[14:]
    x, y, co = lax.axis_index("x"), lax.axis_index("y"), lax.axis_index("co")
    way = 1 - 2 * co
    half = v_refs[4].shape[0]
    spots = [2 * x, 2 * lax.rem(x + 3, NX), 2 * lax.rem(x + 1, NX)]
    far = 2 * lax.rem(x + 2, NX)
    to = [a_all.at[pl.ds(s, 2)] for s in spots] + [a_all.at[far], a_all.at[far + 1]]
    copies = [pltpu.make_async_copy(r, t, sems.at[i]) for i, (r, t) in enumerate(zip(a_refs, to))]
    for copy in copies:
        copy.start()
    for copy in copies:
        copy.wait()

    def columns(step):
        at = lax.rem(y - way * step + NY, NY)
        return jnp.concatenate([a_all[at, j] for j in range(3)], axis=1)

    total = jnp.zeros(w_ref.shape, F32)
    for step, i in ((0, 0), (1, 1), (-1, 5), (2, 2), (-2, 6), (3, 3), (-3, 7)):
        total += jnp.dot(columns(step), v_refs[i][...], preferred_element_type=F32)
    a, mine, mates = columns(4), v_refs[4][...], v_refs[8][...]
    low, high = jnp.where(co == 0, mine, mates), jnp.where(co == 0, mates, mine)
    total += jnp.dot(a[:, :half], low, preferred_element_type=F32)
    total += jnp.dot(a[:, half:], high, preferred_element_type=F32)
    w_ref[...] = total
    wt_ref[...] = total.T.reshape(wt_ref.shape).astype(BF16)


def second_kernel(w_ref, *refs):
    s_ref = refs[-1]
    x = lax.axis_index("x")
    for s in range(NX):
        s_ref[lax.rem(x + (NX - s), NX)] = jnp.dot(w_ref[...], refs[s][...], preferred_element_type=F32)


def whole(amplitudes, integrals, dressing):
    rows, wide = amplitudes.shape
    deep = dressing.shape[0] // NX
    zh, co, x = lax.axis_index("zh"), lax.axis_index("co"), lax.axis_index("x")

    a = exchange(jnp.broadcast_to(amplitudes[None], (NZL, rows, wide)), "zl")
    a = a.reshape(2, 3, rows, wide)
    ahead, back = permute(a, "x", NX, 1), permute(a, "x", NX, -1)
    a = [a, ahead, back, permute(ahead[0], "x", NX, 1), permute(back[1], "x", NX, -1)]

    far = permute(integrals, "zh", NZH, 1)
    pair = jnp.where(zh == 0, jnp.stack([integrals, far]), jnp.stack([far, integrals]))
    mate = permute(pair, "co", NCO, 1)
    own = jnp.where(co == 0, jnp.stack([pair, mate], 1), jnp.stack([mate, pair], 1))
    own = own.reshape(NZH * NCO * rows, wide)
    one, two = opposed(own, 1), opposed(own, 2)
    three = opposed(two, 1)
    half = own.shape[0] // 2
    four = opposed(lax.dynamic_slice_in_dim(two, co * half, half, 0), 2)
    v = [own, one, two, three, four]
    v += [permute(v[i], "co", NCO, 1) for i in (1, 2, 3, 4)]

    u = [lax.dynamic_slice_in_dim(dressing, x * deep, deep, 0)]
    for s in (1, 2, 3):
        piece = lax.dynamic_slice_in_dim(dressing, lax.rem(x + s, NX) * deep, deep, 0)
        u.append(permute(piece, "x", NX, s))

    first_cycle, wt = pl.pallas_call(
        first_kernel,
        out_shape=(
            jax.ShapeDtypeStruct((rows, wide), F32),
            jax.ShapeDtypeStruct((wide // 8, 8, rows), BF16),
        ),
        in_specs=[VMEM_SPEC] * 14,
        out_specs=(VMEM_SPEC,) * 2,
        scratch_shapes=[pltpu.VMEM((2 * NX, 3, rows, wide), BF16), pltpu.SemaphoreType.DMA((5,))],
        compiler_params=pltpu.CompilerParams(vmem_limit_bytes=16 * 2**20),
        name="first",
    )(*a, *v)

    wt = exchange(wt, ROW)
    wt = wt.reshape(NX, 8, 8, rows).transpose(0, 2, 1, 3).reshape(NX, 1, 8, deep)
    wt = jnp.broadcast_to(wt, (NX, NZL, 8, deep)).reshape(NX * NZL, 8, deep)
    wt = exchange(wt, COL).reshape(NX * NZL * 8, deep)

    part = pl.pallas_call(
        second_kernel,
        out_shape=jax.ShapeDtypeStruct((NX, NX * NZL * 8, dressing.shape[1]), F32),
        in_specs=[VMEM_SPEC] * 5,
        out_specs=VMEM_SPEC,
        compiler_params=pltpu.CompilerParams(vmem_limit_bytes=16 * 2**20),
        name="second",
    )(wt, *u)
    part = exchange(part, "x")
    return first_cycle, jnp.sum(part, axis=0)


def solution(mesh):
    fine = Mesh(mesh.devices.reshape(NY, NZH, NCO, NX, NZL), ROW + COL)
    return jax.shard_map(
        whole,
        mesh=fine,
        in_specs=(P(ROW, COL), P(ROW, COL), P(None, COL)),
        out_specs=(P(ROW, COL), P(ROW, COL)),
        check_vma=False,
    )
```

time: 194 us -> 183 us (0.943)
  starting transfers between devices: 85.5 us -> 99.5 us
  blocking collectives: 46.3 us -> 34.4 us
  local copies, waits for them, and re-layouts: 11.9 us -> 3 us
  Pallas kernels: 7.16 us -> 2.78 us
  waiting for transfers between devices: 37.9 us -> 41.1 us
  other arithmetic: 3.06 us -> 0.74 us
    ppermute x0 -> x4, starting transfers between devices: none -> 16.8 us  [opposed(): return lax.ppermute(value, ('y', 'co'), pairs)]
    all_to_all x3 -> x2, waiting for transfers between devices: 13.8 us -> 0.01 us  [exchange(): return lax.all_to_all(value, axis, 0, 0, tiled=True)]
    ppermute x13, waiting for transfers between devices: 24 us -> 36 us  [permute(): return lax.ppermute(value, axis, shift(n, s))]
    all_to_all x2, blocking collectives: 46.3 us -> 34.4 us  [exchange(): return lax.all_to_all(value, axis, 0, 0, tiled=True)]
    ppermute x13, starting transfers between devices: 61.2 us -> 50.6 us  [permute(): return lax.ppermute(value, axis, shift(n, s))]
    all_to_all x3 -> x2, starting transfers between devices: 24.2 us -> 32.1 us  [exchange(): return lax.all_to_all(value, axis, 0, 0, tiled=True)]
    unnamed x20 -> x4, local copies, waits for them, and re-layouts: 6.56 us -> 0.01 us
    ppermute x0 -> x4, waiting for transfers between devices: none -> 5.11 us  [opposed(): return lax.ppermute(value, ('y', 'co'), pairs)]
  transfers between devices with their start and end apart: 16 -> 19, of which waited for: 7 -> 9; matrix products, arithmetic and copies ran while one was open for 5% -> 0% of each run, Pallas kernels for 0% -> 0%
where the time goes in v2:
time: 183 us; the launch traced here: 182 us
  starting transfers between devices  99.5 us (54%)
  waiting for transfers between devices  41.1 us (22%)
  blocking collectives  34.4 us (19%)
  local copies, waits for them, and re-layouts  3 us (2%)
  Pallas kernels  2.78 us (2%)
    ppermute x13, starting transfers between devices, permute(): return lax.ppermute(value, axis, shift(n, s))  50.6 us
    ppermute x13, waiting for transfers between devices, permute(): return lax.ppermute(value, axis, shift(n, s))  36 us
    all_to_all x2, blocking collectives, exchange(): return lax.all_to_all(value, axis, 0, 0, tiled=True)  34.4 us
    all_to_all x2, starting transfers between devices, exchange(): return lax.all_to_all(value, axis, 0, 0, tiled=True)  32.1 us
    ppermute x4, starting transfers between devices, opposed(): return lax.ppermute(value, ('y', 'co'), pairs)  16.8 us
    ppermute x4, waiting for transfers between devices, opposed(): return lax.ppermute(value, ('y', 'co'), pairs)  5.11 us
  transfers between devices with their start and end apart: 19, of which 9 were waited for; matrix products, arithmetic and copies ran while one was open for 0% of the time, Pallas kernels for 0%

profile of v2, /device:TPU:1, one launch (start us, length us, event | category | flops | bytes accessed | tf_op | source)
XLA Modules:
  0.0 182.5 jit_solution(12296236416189113039)
XLA Ops:
  0.6 0.0 copy-start.1
  0.6 1.8 broadcast_in_dim.6
  2.4 12.6 %all-to-all-start = ((bf16[6,192,256]{2,1,0:T(8,128)(2,1)}), bf16[6,192,256]{2,1,0:T(8,128)(2,1)S(1)}, u32[]{:S(2)}, u32[]{:S(2)}) async-start(bf16[6,192,256]{2,1,0:T(8,128)(2,1)} %broadcast_in_dim.6), calls=%async_computation | async-start | bytes 1179648 | tf_op jit(solution)/shard_map/all_to_all | solution.py:32
  15.0 0.0 copy-done.1
  15.1 9.7 %collective-permute-start.4 = (bf16[192,256]{1,0:T(8,128)(2,1)S(1)}, bf16[192,256]{1,0:T(8,128)(2,1)S(1)}, u32[]{:S(2)}, u32[]{:S(2)}) collective-permute-start(bf16[192,256]{1,0:T(8,128)(2,1)S(1)} %copy-done.1), channel_id=1, source_target_pairs={{0,48},{48,0},{1,49},{49,1},{2,50},{50,2},{3,51},{51,3},{4,52},{52... | collective-permute-start | bytes 294920 | tf_op jit(solution)/shard_map/ppermute | solution.py:21
  24.8 11.5 %collective-permute-done.4 = bf16[192,256]{1,0:T(8,128)(2,1)S(1)} collective-permute-done((bf16[192,256]{1,0:T(8,128)(2,1)S(1)}, bf16[192,256]{1,0:T(8,128)(2,1)S(1)}, u32[]{:S(2)}, u32[]{:S(2)}) %collective-permute-start.4) | collective-permute-done | bytes 98336 | tf_op jit(solution)/shard_map/ppermute | solution.py:21
  36.4 4.6 %collective-permute-start.5 = (bf16[2,192,256]{2,1,0:T(8,128)(2,1)S(1)}, bf16[2,192,256]{2,1,0:T(8,128)(2,1)S(1)}, u32[]{:S(2)}, u32[]{:S(2)}) collective-permute-start(bf16[2,192,256]{2,1,0:T(8,128)(2,1)S(1)} %maximum_select_fusion.2), channel_id=1, source_target_pairs={{0,24},{24,0},{1,25},{25,1},{2,26},{26,2},{3,27},{27,3},{4,28},{28... | collective-permute-start | bytes 589832 | tf_op jit(solution)/shard_map/ppermute | solution.py:21
  41.0 1.0 collective-permute-done.5
  42.1 5.9 %collective-permute-start.7 = (bf16[768,256]{1,0:T(8,128)(2,1)S(1)}, bf16[768,256]{1,0:T(8,128)(2,1)S(1)}, u32[]{:S(2)}, u32[]{:S(2)}) collective-permute-start(bf16[768,256]{1,0:T(8,128)(2,1)S(1)} %bitcast.23), channel_id=1, source_target_pairs={{0,192},{24,600},{96,288},{120,696},{192,384},{216,24},{288,480},{... | collective-permute-start | bytes 1179656 | tf_op jit(solution)/shard_map/ppermute | solution.py:28
  48.0 0.0 all-to-all-done
  48.0 3.1 %collective-permute-start = (bf16[2,3,192,256]{3,2,1,0:T(8,128)(2,1)S(1)}, bf16[2,3,192,256]{3,2,1,0:T(8,128)(2,1)S(1)}, u32[]{:S(2)}, u32[]{:S(2)}) collective-permute-start(bf16[2,3,192,256]{3,2,1,0:T(8,128)(2,1)S(1)} %bitcast.20), channel_id=1, source_target_pairs={{0,6},{6,12},{12,18},{18,0},{1,7},{7,13},{13,19},{19,1},{2,8},{8,1... | collective-permute-start | bytes 1769480 | tf_op jit(solution)/shard_map/ppermute | solution.py:21
  51.1 3.0 %collective-permute-start.6 = (bf16[768,256]{1,0:T(8,128)(2,1)S(1)}, bf16[768,256]{1,0:T(8,128)(2,1)S(1)}, u32[]{:S(2)}, u32[]{:S(2)}) collective-permute-start(bf16[768,256]{1,0:T(8,128)(2,1)S(1)} %bitcast.24), channel_id=1, source_target_pairs={{0,96},{24,696},{96,192},{120,24},{192,288},{216,120},{288,384},{3... | collective-permute-start | bytes 1179656 | tf_op jit(solution)/shard_map/ppermute | solution.py:28
  54.1 2.8 %collective-permute-done.7.refs_7_ = bf16[768,256]{1,0:T(8,128)(2,1)S(1)} collective-permute-done((bf16[768,256]{1,0:T(8,128)(2,1)S(1)}, bf16[768,256]{1,0:T(8,128)(2,1)S(1)}, u32[]{:S(2)}, u32[]{:S(2)}) %collective-permute-start.7) | collective-permute-done | bytes 393248 | tf_op jit(solution)/shard_map/ppermute | solution.py:28
  56.9 4.2 %collective-permute-start.8 = (bf16[768,256]{1,0:T(8,128)(2,1)S(1)}, bf16[768,256]{1,0:T(8,128)(2,1)S(1)}, u32[]{:S(2)}, u32[]{:S(2)}) collective-permute-start(bf16[768,256]{1,0:T(8,128)(2,1)S(1)} %collective-permute-done.7.refs_7_), channel_id=1, source_target_pairs={{0,96},{24,696},{96,192},{120,24},{192,288},{216,120},{288,384},{3... | collective-permute-start | bytes 1179656 | tf_op jit(solution)/shard_map/ppermute | solution.py:28
  61.1 4.4 %collective-permute-start.1 = (bf16[2,3,192,256]{3,2,1,0:T(8,128)(2,1)S(1)}, bf16[2,3,192,256]{3,2,1,0:T(8,128)(2,1)S(1)}, u32[]{:S(2)}, u32[]{:S(2)}) collective-permute-start(bf16[2,3,192,256]{3,2,1,0:T(8,128)(2,1)S(1)} %bitcast.21), channel_id=1, source_target_pairs={{0,18},{6,0},{12,6},{18,12},{1,19},{7,1},{13,7},{19,13},{2,20},{8,... | collective-permute-start | bytes 1769480 | tf_op jit(solution)/shard_map/ppermute | solution.py:21
  65.5 3.7 %collective-permute-start.9 = (bf16[384,256]{1,0:T(8,128)(2,1)S(1)}, bf16[384,256]{1,0:T(8,128)(2,1)S(1)}, u32[]{:S(2)}, u32[]{:S(2)}) collective-permute-start(bf16[384,256]{1,0:T(8,128)(2,1)S(1)} %constant_dynamic-slice_fusion.4), channel_id=1, source_target_pairs={{0,192},{24,600},{96,288},{120,696},{192,384},{216,24},{288,480},{... | collective-permute-start | bytes 589832 | tf_op jit(solution)/shard_map/ppermute | solution.py:28
  69.3 0.0 collective-permute-done.6.refs_6_
  69.3 2.6 %collective-permute-start.11 = (bf16[768,256]{1,0:T(8,128)(2,1)S(1)}, bf16[768,256]{1,0:T(8,128)(2,1)S(1)}, u32[]{:S(2)}, u32[]{:S(2)}) collective-permute-start(bf16[768,256]{1,0:T(8,128)(2,1)S(1)} %collective-permute-done.7.refs_7_), channel_id=1, source_target_pairs={{0,24},{24,0},{1,25},{25,1},{2,26},{26,2},{3,27},{27,3},{4,28},{28... | collective-permute-start | bytes 1179656 | tf_op jit(solution)/shard_map/ppermute | solution.py:21
  71.9 2.3 %collective-permute-done.9.refs_9_ = bf16[384,256]{1,0:T(8,128)(2,1)S(1)} collective-permute-done((bf16[384,256]{1,0:T(8,128)(2,1)S(1)}, bf16[384,256]{1,0:T(8,128)(2,1)S(1)}, u32[]{:S(2)}, u32[]{:S(2)}) %collective-permute-start.9) | collective-permute-done | bytes 196640 | tf_op jit(solution)/shard_map/ppermute | solution.py:28
  74.2 4.7 %collective-permute-start.10 = (bf16[768,256]{1,0:T(8,128)(2,1)S(1)}, bf16[768,256]{1,0:T(8,128)(2,1)S(1)}, u32[]{:S(2)}, u32[]{:S(2)}) collective-permute-start(bf16[768,256]{1,0:T(8,128)(2,1)S(1)} %collective-permute-done.6.refs_6_), channel_id=1, source_target_pairs={{0,24},{24,0},{1,25},{25,1},{2,26},{26,2},{3,27},{27,3},{4,28},{28... | collective-permute-start | bytes 1179656 | tf_op jit(solution)/shard_map/ppermute | solution.py:21
  78.9 0.0 collective-permute-done.8.refs_8_
  78.9 1.9 %collective-permute-start.13 = (bf16[384,256]{1,0:T(8,128)(2,1)S(1)}, bf16[384,256]{1,0:T(8,128)(2,1)S(1)}, u32[]{:S(2)}, u32[]{:S(2)}) collective-permute-start(bf16[384,256]{1,0:T(8,128)(2,1)S(1)} %collective-permute-done.9.refs_9_), channel_id=1, source_target_pairs={{0,24},{24,0},{1,25},{25,1},{2,26},{26,2},{3,27},{27,3},{4,28},{28... | collective-permute-start | bytes 589832 | tf_op jit(solution)/shard_map/ppermute | solution.py:21
  80.8 0.0 collective-permute-done.refs_1_
  80.8 2.4 %collective-permute-start.12 = (bf16[768,256]{1,0:T(8,128)(2,1)S(1)}, bf16[768,256]{1,0:T(8,128)(2,1)S(1)}, u32[]{:S(2)}, u32[]{:S(2)}) collective-permute-start(bf16[768,256]{1,0:T(8,128)(2,1)S(1)} %collective-permute-done.8.refs_8_), channel_id=1, source_target_pairs={{0,24},{24,0},{1,25},{25,1},{2,26},{26,2},{3,27},{27,3},{4,28},{28... | collective-permute-start | bytes 1179656 | tf_op jit(solution)/shard_map/ppermute | solution.py:21
  83.3 0.0 collective-permute-done.1.refs_2_
  83.3 1.9 %collective-permute-start.2 = (bf16[3,192,256]{2,1,0:T(8,128)(2,1)S(1)}, bf16[3,192,256]{2,1,0:T(8,128)(2,1)S(1)}, u32[]{:S(2)}, u32[]{:S(2)}) collective-permute-start(bf16[3,192,256]{2,1,0:T(8,128)(2,1)S(1)} %slice_bitcast_fusion.1), channel_id=1, source_target_pairs={{0,6},{6,12},{12,18},{18,0},{1,7},{7,13},{13,19},{19,1},{2,8},{8,1... | collective-permute-start | bytes 884744 | tf_op jit(solution)/shard_map/ppermute | solution.py:21
  85.3 0.0 collective-permute-done.13.refs_13_
  85.3 4.6 %collective-permute-start.3 = (bf16[3,192,256]{2,1,0:T(8,128)(2,1)S(1)}, bf16[3,192,256]{2,1,0:T(8,128)(2,1)S(1)}, u32[]{:S(2)}, u32[]{:S(2)}) collective-permute-start(bf16[3,192,256]{2,1,0:T(8,128)(2,1)S(1)} %slice_bitcast_fusion), channel_id=1, source_target_pairs={{0,18},{6,0},{12,6},{18,12},{1,19},{7,1},{13,7},{19,13},{2,20},{8,... | collective-permute-start | bytes 884744 | tf_op jit(solution)/shard_map/ppermute | solution.py:21
  89.9 0.0 collective-permute-done.11.refs_11_
  89.9 0.0 collective-permute-done.10.refs_10_
  89.9 0.0 collective-permute-done.12.refs_12_
  89.9 5.1 %collective-permute-done.2.refs_3_ = bf16[3,192,256]{2,1,0:T(8,128)(2,1)S(1)} collective-permute-done((bf16[3,192,256]{2,1,0:T(8,128)(2,1)S(1)}, bf16[3,192,256]{2,1,0:T(8,128)(2,1)S(1)}, u32[]{:S(2)}, u32[]{:S(2)}) %collective-permute-start.2) | collective-permute-done | bytes 294944 | tf_op jit(solution)/shard_map/ppermute | solution.py:21
  95.0 0.9 collective-permute-done.3.refs_4_
  95.9 2.0 %first.1 = (f32[192,256]{1,0:T(8,128)}, bf16[32,8,192]{2,1,0:T(8,128)(2,1)S(1)}) custom-call(bf16[2,3,192,256]{3,2,1,0:T(8,128)(2,1)S(1)} %bitcast.22, bf16[2,3,192,256]{3,2,1,0:T(8,128)(2,1)S(1)} %collective-permute-done.refs_1_, bf16[2,3,192,256]{3,2,1,0:T(8,128)(2,1)S(1)} %collective-permute-done.1.refs_2_, ...), custom_call_target="tpu_custom_call" | custom-call | tf_op jit(solution)/shard_map/first/pallas_call | solution.py:98
  97.9 0.0 copy-start
  97.9 23.0 %all_to_all.20 = bf16[32,8,192]{2,1,0:T(8,128)(2,1)S(1)} all-to-all(bf16[32,8,192]{2,1,0:T(8,128)(2,1)S(1)} %get-tuple-element.5), channel_id=1, replica_groups=mesh['y'=8,'zh'=2,'co'=2,'x'=4,'zl'=6] {'y','zh','co'}, dimensions={0} | all-to-all | bytes 196608 | tf_op jit(solution)/shard_map/all_to_all | solution.py:32
  121.0 0.1 broadcast_in_dim.14
  121.1 0.9 broadcast_in_dim.15
  122.0 19.5 %all-to-all-start.2 = ((bf16[24,8,1536]{2,1,0:T(8,128)(2,1)}), bf16[24,8,1536]{2,1,0:T(8,128)(2,1)S(1)}, u32[]{:S(2)}, u32[]{:S(2)}) async-start(bf16[24,8,1536]{2,1,0:T(8,128)(2,1)} %bitcast.11), calls=%async_computation.2 | async-start | bytes 1179648 | tf_op jit(solution)/shard_map/all_to_all | solution.py:32
  141.5 0.0 copy-done
  141.5 0.1 constant_dynamic-slice_fusion
  141.6 3.2 %collective-permute-start.14 = (bf16[1536,128]{1,0:T(8,128)(2,1)S(1)}, bf16[1536,128]{1,0:T(8,128)(2,1)S(1)}, u32[]{:S(2)}, u32[]{:S(2)}) collective-permute-start(bf16[1536,128]{1,0:T(8,128)(2,1)S(1)} %get-tuple-element.7), channel_id=1, source_target_pairs={{0,6},{6,12},{12,18},{18,0},{1,7},{7,13},{13,19},{19,1},{2,8},{8,1... | collective-permute-start | bytes 1179656 | tf_op jit(solution)/shard_map/ppermute | solution.py:21
  144.8 4.3 %collective-permute-start.15 = (bf16[1536,128]{1,0:T(8,128)(2,1)S(1)}, bf16[1536,128]{1,0:T(8,128)(2,1)S(1)}, u32[]{:S(2)}, u32[]{:S(2)}) collective-permute-start(bf16[1536,128]{1,0:T(8,128)(2,1)S(1)} %get-tuple-element.9), channel_id=1, source_target_pairs={{0,12},{6,18},{12,0},{18,6},{1,13},{7,19},{13,1},{19,7},{2,14},{8,... | collective-permute-start | bytes 1179656 | tf_op jit(solution)/shard_map/ppermute | solution.py:21
  149.2 3.1 %collective-permute-start.16 = (bf16[1536,128]{1,0:T(8,128)(2,1)S(1)}, bf16[1536,128]{1,0:T(8,128)(2,1)S(1)}, u32[]{:S(2)}, u32[]{:S(2)}) collective-permute-start(bf16[1536,128]{1,0:T(8,128)(2,1)S(1)} %get-tuple-element.6), channel_id=1, source_target_pairs={{0,18},{6,0},{12,6},{18,12},{1,19},{7,1},{13,7},{19,13},{2,20},{8,... | collective-permute-start | bytes 1179656 | tf_op jit(solution)/shard_map/ppermute | solution.py:21
  152.3 6.4 %collective-permute-done.14.refs_1_ = bf16[1536,128]{1,0:T(8,128)(2,1)S(1)} collective-permute-done((bf16[1536,128]{1,0:T(8,128)(2,1)S(1)}, bf16[1536,128]{1,0:T(8,128)(2,1)S(1)}, u32[]{:S(2)}, u32[]{:S(2)}) %collective-permute-start.14) | collective-permute-done | bytes 393248 | tf_op jit(solution)/shard_map/ppermute | solution.py:21
  158.7 10.2 %collective-permute-done.15.refs_2_ = bf16[1536,128]{1,0:T(8,128)(2,1)S(1)} collective-permute-done((bf16[1536,128]{1,0:T(8,128)(2,1)S(1)}, bf16[1536,128]{1,0:T(8,128)(2,1)S(1)}, u32[]{:S(2)}, u32[]{:S(2)}) %collective-permute-start.15) | collective-permute-done | bytes 393248 | tf_op jit(solution)/shard_map/ppermute | solution.py:21
  168.9 0.7 collective-permute-done.16.refs_3_
  169.7 0.0 all-to-all-done.2
  169.7 0.8 second.1
  170.4 11.4 %all_to_all.21 = f32[4,192,128]{2,1,0:T(8,128)S(1)} all-to-all(f32[4,192,128]{2,1,0:T(8,128)S(1)} %second.1), channel_id=1, replica_groups=mesh['y'=8,'zh'=2,'co'=2,'x'=4,'zl'=6] {'x'}, dimensions={0} | all-to-all | bytes 786432 | tf_op jit(solution)/shard_map/all_to_all | solution.py:32
  181.8 0.7 reduce_sum.9
  (7 shorter events, 0.2 us)
Async XLA Ops:
  0.6 14.4 %copy-start.1 = (bf16[192,256]{1,0:T(8,128)(2,1)S(1)}, bf16[192,256]{1,0:T(8,128)(2,1)}, u32[]{:S(2)}) copy-start(bf16[192,256]{1,0:T(8,128)(2,1)} %param.4) | copy-start | bytes 294916
  2.4 45.6 %all-to-all-start = ((bf16[6,192,256]{2,1,0:T(8,128)(2,1)}), bf16[6,192,256]{2,1,0:T(8,128)(2,1)S(1)}, u32[]{:S(2)}, u32[]{:S(2)}) async-start(bf16[6,192,256]{2,1,0:T(8,128)(2,1)} %broadcast_in_dim.6), calls=%async_computation | async-start | bytes 1179648 | tf_op jit(solution)/shard_map/all_to_all | solution.py:32
  15.1 21.3 %collective-permute-start.4 = (bf16[192,256]{1,0:T(8,128)(2,1)S(1)}, bf16[192,256]{1,0:T(8,128)(2,1)S(1)}, u32[]{:S(2)}, u32[]{:S(2)}) collective-permute-start(bf16[192,256]{1,0:T(8,128)(2,1)S(1)} %copy-done.1), channel_id=1, source_target_pairs={{0,48},{48,0},{1,49},{49,1},{2,50},{50,2},{3,51},{51,3},{4,52},{52... | collective-permute-start | bytes 294920 | tf_op jit(solution)/shard_map/ppermute | solution.py:21
  36.4 5.7 %collective-permute-start.5 = (bf16[2,192,256]{2,1,0:T(8,128)(2,1)S(1)}, bf16[2,192,256]{2,1,0:T(8,128)(2,1)S(1)}, u32[]{:S(2)}, u32[]{:S(2)}) collective-permute-start(bf16[2,192,256]{2,1,0:T(8,128)(2,1)S(1)} %maximum_select_fusion.2), channel_id=1, source_target_pairs={{0,24},{24,0},{1,25},{25,1},{2,26},{26,2},{3,27},{27,3},{4,28},{28... | collective-permute-start | bytes 589832 | tf_op jit(solution)/shard_map/ppermute | solution.py:21
  42.1 14.8 %collective-permute-start.7 = (bf16[768,256]{1,0:T(8,128)(2,1)S(1)}, bf16[768,256]{1,0:T(8,128)(2,1)S(1)}, u32[]{:S(2)}, u32[]{:S(2)}) collective-permute-start(bf16[768,256]{1,0:T(8,128)(2,1)S(1)} %bitcast.23), channel_id=1, source_target_pairs={{0,192},{24,600},{96,288},{120,696},{192,384},{216,24},{288,480},{... | collective-permute-start | bytes 1179656 | tf_op jit(solution)/shard_map/ppermute | solution.py:28
  48.0 32.8 %collective-permute-start = (bf16[2,3,192,256]{3,2,1,0:T(8,128)(2,1)S(1)}, bf16[2,3,192,256]{3,2,1,0:T(8,128)(2,1)S(1)}, u32[]{:S(2)}, u32[]{:S(2)}) collective-permute-start(bf16[2,3,192,256]{3,2,1,0:T(8,128)(2,1)S(1)} %bitcast.20), channel_id=1, source_target_pairs={{0,6},{6,12},{12,18},{18,0},{1,7},{7,13},{13,19},{19,1},{2,8},{8,1... | collective-permute-start | bytes 1769480 | tf_op jit(solution)/shard_map/ppermute | solution.py:21
  51.1 18.2 %collective-permute-start.6 = (bf16[768,256]{1,0:T(8,128)(2,1)S(1)}, bf16[768,256]{1,0:T(8,128)(2,1)S(1)}, u32[]{:S(2)}, u32[]{:S(2)}) collective-permute-start(bf16[768,256]{1,0:T(8,128)(2,1)S(1)} %bitcast.24), channel_id=1, source_target_pairs={{0,96},{24,696},{96,192},{120,24},{192,288},{216,120},{288,384},{3... | collective-permute-start | bytes 1179656 | tf_op jit(solution)/shard_map/ppermute | solution.py:28
  56.9 22.0 %collective-permute-start.8 = (bf16[768,256]{1,0:T(8,128)(2,1)S(1)}, bf16[768,256]{1,0:T(8,128)(2,1)S(1)}, u32[]{:S(2)}, u32[]{:S(2)}) collective-permute-start(bf16[768,256]{1,0:T(8,128)(2,1)S(1)} %collective-permute-done.7.refs_7_), channel_id=1, source_target_pairs={{0,96},{24,696},{96,192},{120,24},{192,288},{216,120},{288,384},{3... | collective-permute-start | bytes 1179656 | tf_op jit(solution)/shard_map/ppermute | solution.py:28
  61.1 22.2 %collective-permute-start.1 = (bf16[2,3,192,256]{3,2,1,0:T(8,128)(2,1)S(1)}, bf16[2,3,192,256]{3,2,1,0:T(8,128)(2,1)S(1)}, u32[]{:S(2)}, u32[]{:S(2)}) collective-permute-start(bf16[2,3,192,256]{3,2,1,0:T(8,128)(2,1)S(1)} %bitcast.21), channel_id=1, source_target_pairs={{0,18},{6,0},{12,6},{18,12},{1,19},{7,1},{13,7},{19,13},{2,20},{8,... | collective-permute-start | bytes 1769480 | tf_op jit(solution)/shard_map/ppermute | solution.py:21
  65.5 8.6 %collective-permute-start.9 = (bf16[384,256]{1,0:T(8,128)(2,1)S(1)}, bf16[384,256]{1,0:T(8,128)(2,1)S(1)}, u32[]{:S(2)}, u32[]{:S(2)}) collective-permute-start(bf16[384,256]{1,0:T(8,128)(2,1)S(1)} %constant_dynamic-slice_fusion.4), channel_id=1, source_target_pairs={{0,192},{24,600},{96,288},{120,696},{192,384},{216,24},{288,480},{... | collective-permute-start | bytes 589832 | tf_op jit(solution)/shard_map/ppermute | solution.py:28
  69.3 20.6 %collective-permute-start.11 = (bf16[768,256]{1,0:T(8,128)(2,1)S(1)}, bf16[768,256]{1,0:T(8,128)(2,1)S(1)}, u32[]{:S(2)}, u32[]{:S(2)}) collective-permute-start(bf16[768,256]{1,0:T(8,128)(2,1)S(1)} %collective-permute-done.7.refs_7_), channel_id=1, source_target_pairs={{0,24},{24,0},{1,25},{25,1},{2,26},{26,2},{3,27},{27,3},{4,28},{28... | collective-permute-start | bytes 1179656 | tf_op jit(solution)/shard_map/ppermute | solution.py:21
  74.2 15.7 %collective-permute-start.10 = (bf16[768,256]{1,0:T(8,128)(2,1)S(1)}, bf16[768,256]{1,0:T(8,128)(2,1)S(1)}, u32[]{:S(2)}, u32[]{:S(2)}) collective-permute-start(bf16[768,256]{1,0:T(8,128)(2,1)S(1)} %collective-permute-done.6.refs_6_), channel_id=1, source_target_pairs={{0,24},{24,0},{1,25},{25,1},{2,26},{26,2},{3,27},{27,3},{4,28},{28... | collective-permute-start | bytes 1179656 | tf_op jit(solution)/shard_map/ppermute | solution.py:21
  78.9 6.4 %collective-permute-start.13 = (bf16[384,256]{1,0:T(8,128)(2,1)S(1)}, bf16[384,256]{1,0:T(8,128)(2,1)S(1)}, u32[]{:S(2)}, u32[]{:S(2)}) collective-permute-start(bf16[384,256]{1,0:T(8,128)(2,1)S(1)} %collective-permute-done.9.refs_9_), channel_id=1, source_target_pairs={{0,24},{24,0},{1,25},{25,1},{2,26},{26,2},{3,27},{27,3},{4,28},{28... | collective-permute-start | bytes 589832 | tf_op jit(solution)/shard_map/ppermute | solution.py:21
  80.8 9.0 %collective-permute-start.12 = (bf16[768,256]{1,0:T(8,128)(2,1)S(1)}, bf16[768,256]{1,0:T(8,128)(2,1)S(1)}, u32[]{:S(2)}, u32[]{:S(2)}) collective-permute-start(bf16[768,256]{1,0:T(8,128)(2,1)S(1)} %collective-permute-done.8.refs_8_), channel_id=1, source_target_pairs={{0,24},{24,0},{1,25},{25,1},{2,26},{26,2},{3,27},{27,3},{4,28},{28... | collective-permute-start | bytes 1179656 | tf_op jit(solution)/shard_map/ppermute | solution.py:21
  83.3 11.7 %collective-permute-start.2 = (bf16[3,192,256]{2,1,0:T(8,128)(2,1)S(1)}, bf16[3,192,256]{2,1,0:T(8,128)(2,1)S(1)}, u32[]{:S(2)}, u32[]{:S(2)}) collective-permute-start(bf16[3,192,256]{2,1,0:T(8,128)(2,1)S(1)} %slice_bitcast_fusion.1), channel_id=1, source_target_pairs={{0,6},{6,12},{12,18},{18,0},{1,7},{7,13},{13,19},{19,1},{2,8},{8,1... | collective-permute-start | bytes 884744 | tf_op jit(solution)/shard_map/ppermute | solution.py:21
  85.3 10.6 %collective-permute-start.3 = (bf16[3,192,256]{2,1,0:T(8,128)(2,1)S(1)}, bf16[3,192,256]{2,1,0:T(8,128)(2,1)S(1)}, u32[]{:S(2)}, u32[]{:S(2)}) collective-permute-start(bf16[3,192,256]{2,1,0:T(8,128)(2,1)S(1)} %slice_bitcast_fusion), channel_id=1, source_target_pairs={{0,18},{6,0},{12,6},{18,12},{1,19},{7,1},{13,7},{19,13},{2,20},{8,... | collective-permute-start | bytes 884744 | tf_op jit(solution)/shard_map/ppermute | solution.py:21
  97.9 43.6 %copy-start = (bf16[6144,128]{1,0:T(8,128)(2,1)S(1)}, bf16[6144,128]{1,0:T(8,128)(2,1)}, u32[]{:S(2)}) copy-start(bf16[6144,128]{1,0:T(8,128)(2,1)} %param.5) | copy-start | bytes 4718596
  122.0 47.7 %all-to-all-start.2 = ((bf16[24,8,1536]{2,1,0:T(8,128)(2,1)}), bf16[24,8,1536]{2,1,0:T(8,128)(2,1)S(1)}, u32[]{:S(2)}, u32[]{:S(2)}) async-start(bf16[24,8,1536]{2,1,0:T(8,128)(2,1)} %bitcast.11), calls=%async_computation.2 | async-start | bytes 1179648 | tf_op jit(solution)/shard_map/all_to_all | solution.py:32
  141.6 17.1 %collective-permute-start.14 = (bf16[1536,128]{1,0:T(8,128)(2,1)S(1)}, bf16[1536,128]{1,0:T(8,128)(2,1)S(1)}, u32[]{:S(2)}, u32[]{:S(2)}) collective-permute-start(bf16[1536,128]{1,0:T(8,128)(2,1)S(1)} %get-tuple-element.7), channel_id=1, source_target_pairs={{0,6},{6,12},{12,18},{18,0},{1,7},{7,13},{13,19},{19,1},{2,8},{8,1... | collective-permute-start | bytes 1179656 | tf_op jit(solution)/shard_map/ppermute | solution.py:21
  144.8 24.1 %collective-permute-start.15 = (bf16[1536,128]{1,0:T(8,128)(2,1)S(1)}, bf16[1536,128]{1,0:T(8,128)(2,1)S(1)}, u32[]{:S(2)}, u32[]{:S(2)}) collective-permute-start(bf16[1536,128]{1,0:T(8,128)(2,1)S(1)} %get-tuple-element.9), channel_id=1, source_target_pairs={{0,12},{6,18},{12,0},{18,6},{1,13},{7,19},{13,1},{19,7},{2,14},{8,... | collective-permute-start | bytes 1179656 | tf_op jit(solution)/shard_map/ppermute | solution.py:21
  149.2 20.5 %collective-permute-start.16 = (bf16[1536,128]{1,0:T(8,128)(2,1)S(1)}, bf16[1536,128]{1,0:T(8,128)(2,1)S(1)}, u32[]{:S(2)}, u32[]{:S(2)}) collective-permute-start(bf16[1536,128]{1,0:T(8,128)(2,1)S(1)} %get-tuple-element.6), channel_id=1, source_target_pairs={{0,18},{6,0},{12,6},{18,12},{1,19},{7,1},{13,7},{19,13},{2,20},{8,... | collective-permute-start | bytes 1179656 | tf_op jit(solution)/shard_map/ppermute | solution.py:21

commit v3 on v2

--- a/solution.py
+++ b/solution.py
@@ -33,9 +33,11 @@
 
 
 def first_kernel(*refs):
-    a_refs, v_refs, (w_ref, wt_ref, a_all, sems) = refs[:5], refs[5:14], refs[14:]
+    a_refs, v_refs, (w_ref, wt_ref, a_all, v_far, sems) = refs[:5], refs[5:14], refs[14:]
     x, y, co = lax.axis_index("x"), lax.axis_index("y"), lax.axis_index("co")
+    spot = lax.rem(lax.axis_index("zl"), 3)
     way = 1 - 2 * co
+    wide = w_ref.shape[1]
     half = v_refs[4].shape[0]
     spots = [2 * x, 2 * lax.rem(x + 3, NX), 2 * lax.rem(x + 1, NX)]
     far = 2 * lax.rem(x + 2, NX)
@@ -43,20 +45,18 @@
     copies = [pltpu.make_async_copy(r, t, sems.at[i]) for i, (r, t) in enumerate(zip(a_refs, to))]
     for copy in copies:
         copy.start()
+    v_far[pl.ds(pl.multiple_of(co * half, half), half)] = v_refs[4][...]
+    v_far[pl.ds(pl.multiple_of((1 - co) * half, half), half)] = v_refs[8][...]
     for copy in copies:
         copy.wait()
 
-    def columns(step):
+    total = jnp.zeros(w_ref.shape, F32)
+    v_all = {0: v_refs[0], 1: v_refs[1], -1: v_refs[5], 2: v_refs[2], -2: v_refs[6], 3: v_refs[3], -3: v_refs[7], 4: v_far}
+    for step, v_ref in v_all.items():
         at = lax.rem(y - way * step + NY, NY)
-        return jnp.concatenate([a_all[at, j] for j in range(3)], axis=1)
-
-    total = jnp.zeros(w_ref.shape, F32)
-    for step, i in ((0, 0), (1, 1), (-1, 5), (2, 2), (-2, 6), (3, 3), (-3, 7)):
-        total += jnp.dot(columns(step), v_refs[i][...], preferred_element_type=F32)
-    a, mine, mates = columns(4), v_refs[4][...], v_refs[8][...]
-    low, high = jnp.where(co == 0, mine, mates), jnp.where(co == 0, mates, mine)
-    total += jnp.dot(a[:, :half], low, preferred_element_type=F32)
-    total += jnp.dot(a[:, half:], high, preferred_element_type=F32)
+        for j in range(3):
+            start = pl.multiple_of(lax.rem(spot + 3 - j, 3) * wide, wide)
+            total += jnp.dot(a_all[at, j], v_ref[pl.ds(start, wide)], preferred_element_type=F32)
     w_ref[...] = total
     wt_ref[...] = total.T.reshape(wt_ref.shape).astype(BF16)
 
@@ -71,10 +71,14 @@
 def whole(amplitudes, integrals, dressing):
     rows, wide = amplitudes.shape
     deep = dressing.shape[0] // NX
-    zh, co, x = lax.axis_index("zh"), lax.axis_index("co"), lax.axis_index("x")
+    zh, co, x, zl = (lax.axis_index(n) for n in ("zh", "co", "x", "zl"))
 
-    a = exchange(jnp.broadcast_to(amplitudes[None], (NZL, rows, wide)), "zl")
-    a = a.reshape(2, 3, rows, wide)
+    far = permute(amplitudes, "zl", NZL, 3)
+    a = jnp.where(zl < 3, jnp.stack([amplitudes, far]), jnp.stack([far, amplitudes]))
+    turns = [[(i, i // 3 * 3 + (i + s) % 3) for i in range(NZL)] for s in (1, 2)]
+    a1 = lax.ppermute(a, "zl", turns[0])
+    a2 = lax.ppermute(a, "zl", turns[1])
+    a = jnp.stack([a, a1, a2], 1)
     ahead, back = permute(a, "x", NX, 1), permute(a, "x", NX, -1)
     a = [a, ahead, back, permute(ahead[0], "x", NX, 1), permute(back[1], "x", NX, -1)]
 
@@ -103,7 +107,7 @@
         ),
         in_specs=[VMEM_SPEC] * 14,
         out_specs=(VMEM_SPEC,) * 2,
-        scratch_shapes=[pltpu.VMEM((2 * NX, 3, rows, wide), BF16), pltpu.SemaphoreType.DMA((5,))],
+        scratch_shapes=[pltpu.VMEM((2 * NX, 3, rows, wide), BF16), pltpu.VMEM(own.shape, BF16), pltpu.SemaphoreType.DMA((5,))],
         compiler_params=pltpu.CompilerParams(vmem_limit_bytes=16 * 2**20),
         name="first",
     )(*a, *v)

time: 183 us -> 176 us (0.962)
  waiting for transfers between devices: 41.1 us -> 29.6 us
  blocking collectives: 34.4 us -> 41 us
  starting transfers between devices: 99.5 us -> 94.4 us
  other arithmetic: 0.74 us -> 4.75 us
    all_to_all x2 -> x1, starting transfers between devices: 32.1 us -> 9.72 us  [exchange(): return lax.all_to_all(value, axis, 0, 0, tiled=True)]
    ppermute x13 -> x14, waiting for transfers between devices: 36 us -> 24 us  [permute(): return lax.ppermute(value, axis, shift(n, s))]
    ppermute x13 -> x14, starting transfers between devices: 50.6 us -> 61.7 us  [permute(): return lax.ppermute(value, axis, shift(n, s))]
    all_to_all x2, blocking collectives: 34.4 us -> 41 us  [exchange(): return lax.all_to_all(value, axis, 0, 0, tiled=True)]
    ppermute x0 -> x2, starting transfers between devices: none -> 6.18 us  [the longest x1 3.69 us: whole(): a2 = lax.ppermute(a, 'zl', turns[1])]
    ppermute x0 -> x2, waiting for transfers between devices: none -> 2.59 us  [the longest x1 2.59 us: whole(): a2 = lax.ppermute(a, 'zl', turns[1])]
    ppermute x4, waiting for transfers between devices: 5.11 us -> 3 us  [opposed(): return lax.ppermute(value, ('y', 'co'), pairs)]
    select_n x0 -> x2, other arithmetic: none -> 1.99 us  [whole(): jnp.where(zl < 3, jnp.stack([amplitudes, far]), jnp.stack([far, amplitude...]
  transfers between devices with their start and end apart: 19 -> 21, of which waited for: 9 -> 7; matrix products, arithmetic and copies ran while one was open for 0% -> 2% of each run, Pallas kernels for 0% -> 0%
where the time goes in v3:
time: 176 us; the launch traced here: 175 us
  starting transfers between devices  94.4 us (54%)
  blocking collectives  41 us (23%)
  waiting for transfers between devices  29.6 us (17%)
  other arithmetic  4.75 us (3%)
  Pallas kernels  2.79 us (2%)
    ppermute x14, starting transfers between devices, permute(): return lax.ppermute(value, axis, shift(n, s))  61.7 us
    all_to_all x2, blocking collectives, exchange(): return lax.all_to_all(value, axis, 0, 0, tiled=True)  41 us
    ppermute x14, waiting for transfers between devices, permute(): return lax.ppermute(value, axis, shift(n, s))  24 us
    ppermute x4, starting transfers between devices, opposed(): return lax.ppermute(value, ('y', 'co'), pairs)  16.8 us
    all_to_all x1, starting transfers between devices, exchange(): return lax.all_to_all(value, axis, 0, 0, tiled=True)  9.72 us
    ppermute x1, starting transfers between devices, whole(): a2 = lax.ppermute(a, 'zl', turns[1])  3.69 us
  transfers between devices with their start and end apart: 21, of which 7 were waited for; matrix products, arithmetic and copies ran while one was open for 2% of the time, Pallas kernels for 0%

profile of v3, /device:TPU:1, one launch (start us, length us, event | category | flops | bytes accessed | tf_op | source)
XLA Modules:
  0.0 174.8 jit_solution(8591041837296833761)
XLA Ops:
  0.6 8.4 %collective-permute-start = (bf16[192,256]{1,0:T(8,128)(2,1)}, bf16[192,256]{1,0:T(8,128)(2,1)S(1)}, u32[]{:S(2)}, u32[]{:S(2)}) collective-permute-start(bf16[192,256]{1,0:T(8,128)(2,1)} %param.3), channel_id=1, source_target_pairs={{0,3},{1,4},{2,5},{3,0},{4,1},{5,2},{6,9},{7,10},{8,11},{9,6},{10,... | collective-permute-start | bytes 294920 | tf_op jit(solution)/shard_map/ppermute | solution.py:21
  9.1 12.8 %collective-permute-start.7 = (bf16[192,256]{1,0:T(8,128)(2,1)}, bf16[192,256]{1,0:T(8,128)(2,1)S(1)}, u32[]{:S(2)}, u32[]{:S(2)}) collective-permute-start(bf16[192,256]{1,0:T(8,128)(2,1)} %param.4), channel_id=1, source_target_pairs={{0,48},{48,0},{1,49},{49,1},{2,50},{50,2},{3,51},{51,3},{4,52},{52... | collective-permute-start | bytes 294920 | tf_op jit(solution)/shard_map/ppermute | solution.py:21
  21.9 0.0 collective-permute-done
  21.9 1.0 maximum_select_fusion.2
  22.9 2.5 %collective-permute-start.1 = (bf16[2,192,256]{2,1,0:T(8,128)(2,1)S(1)}, bf16[2,192,256]{2,1,0:T(8,128)(2,1)S(1)}, u32[]{:S(2)}, u32[]{:S(2)}) collective-permute-start(bf16[2,192,256]{2,1,0:T(8,128)(2,1)S(1)} %maximum_select_fusion.2), channel_id=1, source_target_pairs={{0,1},{1,2},{2,0},{3,4},{4,5},{5,3},{6,7},{7,8},{8,6},{9,10},{10,1... | collective-permute-start | bytes 589832 | tf_op jit(solution)/shard_map/ppermute | solution.py:79
  25.4 3.7 %collective-permute-start.2 = (bf16[2,192,256]{2,1,0:T(8,128)(2,1)S(1)}, bf16[2,192,256]{2,1,0:T(8,128)(2,1)S(1)}, u32[]{:S(2)}, u32[]{:S(2)}) collective-permute-start(bf16[2,192,256]{2,1,0:T(8,128)(2,1)S(1)} %maximum_select_fusion.2), channel_id=1, source_target_pairs={{0,2},{1,0},{2,1},{3,5},{4,3},{5,4},{6,8},{7,6},{8,7},{9,11},{10,9... | collective-permute-start | bytes 589832 | tf_op jit(solution)/shard_map/ppermute | solution.py:80
  29.1 0.0 collective-permute-done.7
  29.1 1.0 maximum_select_fusion.4
  30.1 3.7 %collective-permute-start.8 = (bf16[2,192,256]{2,1,0:T(8,128)(2,1)S(1)}, bf16[2,192,256]{2,1,0:T(8,128)(2,1)S(1)}, u32[]{:S(2)}, u32[]{:S(2)}) collective-permute-start(bf16[2,192,256]{2,1,0:T(8,128)(2,1)S(1)} %maximum_select_fusion.4), channel_id=1, source_target_pairs={{0,24},{24,0},{1,25},{25,1},{2,26},{26,2},{3,27},{27,3},{4,28},{28... | collective-permute-start | bytes 589832 | tf_op jit(solution)/shard_map/ppermute | solution.py:21
  33.8 1.0 maximum_select_fusion.3
  34.8 1.0 maximum_select_fusion.1
  35.8 0.0 collective-permute-done.1
  35.8 2.6 %collective-permute-done.2 = bf16[2,192,256]{2,1,0:T(8,128)(2,1)S(1)} collective-permute-done((bf16[2,192,256]{2,1,0:T(8,128)(2,1)S(1)}, bf16[2,192,256]{2,1,0:T(8,128)(2,1)S(1)}, u32[]{:S(2)}, u32[]{:S(2)}) %collective-permute-start.2) | collective-permute-done | bytes 196640 | tf_op jit(solution)/shard_map/ppermute | solution.py:80
  38.4 0.1 pad_maximum_fusion.refs_0_
  38.5 3.1 %collective-permute-start.3 = (bf16[2,3,192,256]{3,2,1,0:T(8,128)(2,1)S(1)}, bf16[2,3,192,256]{3,2,1,0:T(8,128)(2,1)S(1)}, u32[]{:S(2)}, u32[]{:S(2)}) collective-permute-start(bf16[2,3,192,256]{3,2,1,0:T(8,128)(2,1)S(1)} %pad_maximum_fusion.refs_0_), channel_id=1, source_target_pairs={{0,6},{6,12},{12,18},{18,0},{1,7},{7,13},{13,19},{19,1},{2,8},{8,1... | collective-permute-start | bytes 1769480 | tf_op jit(solution)/shard_map/ppermute | solution.py:21
  41.6 0.0 collective-permute-done.8
  41.7 5.9 %collective-permute-start.10 = (bf16[768,256]{1,0:T(8,128)(2,1)S(1)}, bf16[768,256]{1,0:T(8,128)(2,1)S(1)}, u32[]{:S(2)}, u32[]{:S(2)}) collective-permute-start(bf16[768,256]{1,0:T(8,128)(2,1)S(1)} %bitcast.27), channel_id=1, source_target_pairs={{0,192},{24,600},{96,288},{120,696},{192,384},{216,24},{288,480},{... | collective-permute-start | bytes 1179656 | tf_op jit(solution)/shard_map/ppermute | solution.py:28
  47.5 3.0 %collective-permute-start.9 = (bf16[768,256]{1,0:T(8,128)(2,1)S(1)}, bf16[768,256]{1,0:T(8,128)(2,1)S(1)}, u32[]{:S(2)}, u32[]{:S(2)}) collective-permute-start(bf16[768,256]{1,0:T(8,128)(2,1)S(1)} %bitcast.28), channel_id=1, source_target_pairs={{0,96},{24,696},{96,192},{120,24},{192,288},{216,120},{288,384},{3... | collective-permute-start | bytes 1179656 | tf_op jit(solution)/shard_map/ppermute | solution.py:28
  50.5 3.4 %collective-permute-start.4 = (bf16[2,3,192,256]{3,2,1,0:T(8,128)(2,1)S(1)}, bf16[2,3,192,256]{3,2,1,0:T(8,128)(2,1)S(1)}, u32[]{:S(2)}, u32[]{:S(2)}) collective-permute-start(bf16[2,3,192,256]{3,2,1,0:T(8,128)(2,1)S(1)} %pad_maximum_fusion.refs_0_), channel_id=1, source_target_pairs={{0,18},{6,0},{12,6},{18,12},{1,19},{7,1},{13,7},{19,13},{2,20},{8,... | collective-permute-start | bytes 1769480 | tf_op jit(solution)/shard_map/ppermute | solution.py:21
  53.9 2.5 %collective-permute-done.10.refs_7_ = bf16[768,256]{1,0:T(8,128)(2,1)S(1)} collective-permute-done((bf16[768,256]{1,0:T(8,128)(2,1)S(1)}, bf16[768,256]{1,0:T(8,128)(2,1)S(1)}, u32[]{:S(2)}, u32[]{:S(2)}) %collective-permute-start.10) | collective-permute-done | bytes 393248 | tf_op jit(solution)/shard_map/ppermute | solution.py:28
  56.5 4.2 %collective-permute-start.11 = (bf16[768,256]{1,0:T(8,128)(2,1)S(1)}, bf16[768,256]{1,0:T(8,128)(2,1)S(1)}, u32[]{:S(2)}, u32[]{:S(2)}) collective-permute-start(bf16[768,256]{1,0:T(8,128)(2,1)S(1)} %collective-permute-done.10.refs_7_), channel_id=1, source_target_pairs={{0,96},{24,696},{96,192},{120,24},{192,288},{216,120},{288,384},{3... | collective-permute-start | bytes 1179656 | tf_op jit(solution)/shard_map/ppermute | solution.py:28
  60.7 3.7 %collective-permute-start.12 = (bf16[384,256]{1,0:T(8,128)(2,1)S(1)}, bf16[384,256]{1,0:T(8,128)(2,1)S(1)}, u32[]{:S(2)}, u32[]{:S(2)}) collective-permute-start(bf16[384,256]{1,0:T(8,128)(2,1)S(1)} %constant_dynamic-slice_fusion.4), channel_id=1, source_target_pairs={{0,192},{24,600},{96,288},{120,696},{192,384},{216,24},{288,480},{... | collective-permute-start | bytes 589832 | tf_op jit(solution)/shard_map/ppermute | solution.py:28
  64.4 0.0 collective-permute-done.9.refs_6_
  64.5 2.7 %collective-permute-start.14 = (bf16[768,256]{1,0:T(8,128)(2,1)S(1)}, bf16[768,256]{1,0:T(8,128)(2,1)S(1)}, u32[]{:S(2)}, u32[]{:S(2)}) collective-permute-start(bf16[768,256]{1,0:T(8,128)(2,1)S(1)} %collective-permute-done.10.refs_7_), channel_id=1, source_target_pairs={{0,24},{24,0},{1,25},{25,1},{2,26},{26,2},{3,27},{27,3},{4,28},{28... | collective-permute-start | bytes 1179656 | tf_op jit(solution)/shard_map/ppermute | solution.py:21
  67.2 0.0 collective-permute-done.3.refs_1_
  67.2 1.9 %collective-permute-start.13 = (bf16[768,256]{1,0:T(8,128)(2,1)S(1)}, bf16[768,256]{1,0:T(8,128)(2,1)S(1)}, u32[]{:S(2)}, u32[]{:S(2)}) collective-permute-start(bf16[768,256]{1,0:T(8,128)(2,1)S(1)} %collective-permute-done.9.refs_6_), channel_id=1, source_target_pairs={{0,24},{24,0},{1,25},{25,1},{2,26},{26,2},{3,27},{27,3},{4,28},{28... | collective-permute-start | bytes 1179656 | tf_op jit(solution)/shard_map/ppermute | solution.py:21
  69.1 0.4 collective-permute-done.12.refs_9_
  69.6 3.1 %collective-permute-start.5 = (bf16[3,192,256]{2,1,0:T(8,128)(2,1)S(1)}, bf16[3,192,256]{2,1,0:T(8,128)(2,1)S(1)}, u32[]{:S(2)}, u32[]{:S(2)}) collective-permute-start(bf16[3,192,256]{2,1,0:T(8,128)(2,1)S(1)} %slice_bitcast_fusion.1), channel_id=1, source_target_pairs={{0,6},{6,12},{12,18},{18,0},{1,7},{7,13},{13,19},{19,1},{2,8},{8,1... | collective-permute-start | bytes 884744 | tf_op jit(solution)/shard_map/ppermute | solution.py:21
  72.7 0.0 collective-permute-done.4.refs_2_
  72.7 6.7 %collective-permute-start.16 = (bf16[384,256]{1,0:T(8,128)(2,1)S(1)}, bf16[384,256]{1,0:T(8,128)(2,1)S(1)}, u32[]{:S(2)}, u32[]{:S(2)}) collective-permute-start(bf16[384,256]{1,0:T(8,128)(2,1)S(1)} %collective-permute-done.12.refs_9_), channel_id=1, source_target_pairs={{0,24},{24,0},{1,25},{25,1},{2,26},{26,2},{3,27},{27,3},{4,28},{28... | collective-permute-start | bytes 589832 | tf_op jit(solution)/shard_map/ppermute | solution.py:21
  79.4 0.0 collective-permute-done.11.refs_8_
  79.4 1.9 %collective-permute-start.15 = (bf16[768,256]{1,0:T(8,128)(2,1)S(1)}, bf16[768,256]{1,0:T(8,128)(2,1)S(1)}, u32[]{:S(2)}, u32[]{:S(2)}) collective-permute-start(bf16[768,256]{1,0:T(8,128)(2,1)S(1)} %collective-permute-done.11.refs_8_), channel_id=1, source_target_pairs={{0,24},{24,0},{1,25},{25,1},{2,26},{26,2},{3,27},{27,3},{4,28},{28... | collective-permute-start | bytes 1179656 | tf_op jit(solution)/shard_map/ppermute | solution.py:21
  81.4 0.0 collective-permute-done.16.refs_13_
  81.4 3.4 %collective-permute-start.6 = (bf16[3,192,256]{2,1,0:T(8,128)(2,1)S(1)}, bf16[3,192,256]{2,1,0:T(8,128)(2,1)S(1)}, u32[]{:S(2)}, u32[]{:S(2)}) collective-permute-start(bf16[3,192,256]{2,1,0:T(8,128)(2,1)S(1)} %slice_bitcast_fusion), channel_id=1, source_target_pairs={{0,18},{6,0},{12,6},{18,12},{1,19},{7,1},{13,7},{19,13},{2,20},{8,... | collective-permute-start | bytes 884744 | tf_op jit(solution)/shard_map/ppermute | solution.py:21
  84.8 0.0 collective-permute-done.14.refs_11_
  84.8 0.0 collective-permute-done.13.refs_10_
  84.8 0.0 collective-permute-done.5.refs_3_
  84.8 6.5 %collective-permute-done.6.refs_4_ = bf16[3,192,256]{2,1,0:T(8,128)(2,1)S(1)} collective-permute-done((bf16[3,192,256]{2,1,0:T(8,128)(2,1)S(1)}, bf16[3,192,256]{2,1,0:T(8,128)(2,1)S(1)}, u32[]{:S(2)}, u32[]{:S(2)}) %collective-permute-start.6) | collective-permute-done | bytes 294944 | tf_op jit(solution)/shard_map/ppermute | solution.py:21
  91.4 0.0 collective-permute-done.15.refs_12_
  91.4 2.0 %first.1 = (f32[192,256]{1,0:T(8,128)}, bf16[32,8,192]{2,1,0:T(8,128)(2,1)S(1)}) custom-call(bf16[2,3,192,256]{3,2,1,0:T(8,128)(2,1)S(1)} %pad_maximum_fusion.refs_0_, bf16[2,3,192,256]{3,2,1,0:T(8,128)(2,1)S(1)} %collective-permute-done.3.refs_1_, bf16[2,3,192,256]{3,2,1,0:T(8,128)(2,1)S(1)} %collective-permute-done.4.refs_2_, ...), custom_call_target="tpu_custom_call" | custom-call | tf_op jit(solution)/shard_map/first/pallas_call | solution.py:102
  93.4 0.0 copy-start
  93.4 29.9 %all_to_all.15 = bf16[32,8,192]{2,1,0:T(8,128)(2,1)S(1)} all-to-all(bf16[32,8,192]{2,1,0:T(8,128)(2,1)S(1)} %get-tuple-element.5), channel_id=1, replica_groups=mesh['y'=8,'zh'=2,'co'=2,'x'=4,'zl'=6] {'y','zh','co'}, dimensions={0} | all-to-all | bytes 196608 | tf_op jit(solution)/shard_map/all_to_all | solution.py:32
  123.3 0.1 broadcast_in_dim.7
  123.5 0.9 broadcast_in_dim.8
  124.3 9.7 %all-to-all-start.1 = ((bf16[24,8,1536]{2,1,0:T(8,128)(2,1)}), bf16[24,8,1536]{2,1,0:T(8,128)(2,1)S(1)}, u32[]{:S(2)}, u32[]{:S(2)}) async-start(bf16[24,8,1536]{2,1,0:T(8,128)(2,1)} %bitcast.17), calls=%async_computation.1 | async-start | bytes 1179648 | tf_op jit(solution)/shard_map/all_to_all | solution.py:32
  134.1 0.0 copy-done
  134.1 0.1 constant_dynamic-slice_fusion
  134.2 3.2 %collective-permute-start.17 = (bf16[1536,128]{1,0:T(8,128)(2,1)S(1)}, bf16[1536,128]{1,0:T(8,128)(2,1)S(1)}, u32[]{:S(2)}, u32[]{:S(2)}) collective-permute-start(bf16[1536,128]{1,0:T(8,128)(2,1)S(1)} %get-tuple-element.7), channel_id=1, source_target_pairs={{0,6},{6,12},{12,18},{18,0},{1,7},{7,13},{13,19},{19,1},{2,8},{8,1... | collective-permute-start | bytes 1179656 | tf_op jit(solution)/shard_map/ppermute | solution.py:21
  137.4 4.3 %collective-permute-start.18 = (bf16[1536,128]{1,0:T(8,128)(2,1)S(1)}, bf16[1536,128]{1,0:T(8,128)(2,1)S(1)}, u32[]{:S(2)}, u32[]{:S(2)}) collective-permute-start(bf16[1536,128]{1,0:T(8,128)(2,1)S(1)} %get-tuple-element.9), channel_id=1, source_target_pairs={{0,12},{6,18},{12,0},{18,6},{1,13},{7,19},{13,1},{19,7},{2,14},{8,... | collective-permute-start | bytes 1179656 | tf_op jit(solution)/shard_map/ppermute | solution.py:21
  141.7 3.1 %collective-permute-start.19 = (bf16[1536,128]{1,0:T(8,128)(2,1)S(1)}, bf16[1536,128]{1,0:T(8,128)(2,1)S(1)}, u32[]{:S(2)}, u32[]{:S(2)}) collective-permute-start(bf16[1536,128]{1,0:T(8,128)(2,1)S(1)} %get-tuple-element.6), channel_id=1, source_target_pairs={{0,18},{6,0},{12,6},{18,12},{1,19},{7,1},{13,7},{19,13},{2,20},{8,... | collective-permute-start | bytes 1179656 | tf_op jit(solution)/shard_map/ppermute | solution.py:21
  144.8 6.8 %collective-permute-done.17.refs_1_ = bf16[1536,128]{1,0:T(8,128)(2,1)S(1)} collective-permute-done((bf16[1536,128]{1,0:T(8,128)(2,1)S(1)}, bf16[1536,128]{1,0:T(8,128)(2,1)S(1)}, u32[]{:S(2)}, u32[]{:S(2)}) %collective-permute-start.17) | collective-permute-done | bytes 393248 | tf_op jit(solution)/shard_map/ppermute | solution.py:21
  151.6 10.0 %collective-permute-done.18.refs_2_ = bf16[1536,128]{1,0:T(8,128)(2,1)S(1)} collective-permute-done((bf16[1536,128]{1,0:T(8,128)(2,1)S(1)}, bf16[1536,128]{1,0:T(8,128)(2,1)S(1)}, u32[]{:S(2)}, u32[]{:S(2)}) %collective-permute-start.18) | collective-permute-done | bytes 393248 | tf_op jit(solution)/shard_map/ppermute | solution.py:21
  161.6 0.6 collective-permute-done.19.refs_3_
  162.2 0.0 all-to-all-done.1
  162.2 0.8 second.1
  163.0 11.1 %all_to_all.16 = f32[4,192,128]{2,1,0:T(8,128)S(1)} all-to-all(f32[4,192,128]{2,1,0:T(8,128)S(1)} %second.1), channel_id=1, replica_groups=mesh['y'=8,'zh'=2,'co'=2,'x'=4,'zl'=6] {'x'}, dimensions={0} | all-to-all | bytes 786432 | tf_op jit(solution)/shard_map/all_to_all | solution.py:32
  174.1 0.7 reduce_sum.9
  (5 shorter events, 0.1 us)
Async XLA Ops:
  0.6 21.2 %collective-permute-start = (bf16[192,256]{1,0:T(8,128)(2,1)}, bf16[192,256]{1,0:T(8,128)(2,1)S(1)}, u32[]{:S(2)}, u32[]{:S(2)}) collective-permute-start(bf16[192,256]{1,0:T(8,128)(2,1)} %param.3), channel_id=1, source_target_pairs={{0,3},{1,4},{2,5},{3,0},{4,1},{5,2},{6,9},{7,10},{8,11},{9,6},{10,... | collective-permute-start | bytes 294920 | tf_op jit(solution)/shard_map/ppermute | solution.py:21
  9.1 20.0 %collective-permute-start.7 = (bf16[192,256]{1,0:T(8,128)(2,1)}, bf16[192,256]{1,0:T(8,128)(2,1)S(1)}, u32[]{:S(2)}, u32[]{:S(2)}) collective-permute-start(bf16[192,256]{1,0:T(8,128)(2,1)} %param.4), channel_id=1, source_target_pairs={{0,48},{48,0},{1,49},{49,1},{2,50},{50,2},{3,51},{51,3},{4,52},{52... | collective-permute-start | bytes 294920 | tf_op jit(solution)/shard_map/ppermute | solution.py:21
  22.9 12.9 %collective-permute-start.1 = (bf16[2,192,256]{2,1,0:T(8,128)(2,1)S(1)}, bf16[2,192,256]{2,1,0:T(8,128)(2,1)S(1)}, u32[]{:S(2)}, u32[]{:S(2)}) collective-permute-start(bf16[2,192,256]{2,1,0:T(8,128)(2,1)S(1)} %maximum_select_fusion.2), channel_id=1, source_target_pairs={{0,1},{1,2},{2,0},{3,4},{4,5},{5,3},{6,7},{7,8},{8,6},{9,10},{10,1... | collective-permute-start | bytes 589832 | tf_op jit(solution)/shard_map/ppermute | solution.py:79
  25.4 13.0 %collective-permute-start.2 = (bf16[2,192,256]{2,1,0:T(8,128)(2,1)S(1)}, bf16[2,192,256]{2,1,0:T(8,128)(2,1)S(1)}, u32[]{:S(2)}, u32[]{:S(2)}) collective-permute-start(bf16[2,192,256]{2,1,0:T(8,128)(2,1)S(1)} %maximum_select_fusion.2), channel_id=1, source_target_pairs={{0,2},{1,0},{2,1},{3,5},{4,3},{5,4},{6,8},{7,6},{8,7},{9,11},{10,9... | collective-permute-start | bytes 589832 | tf_op jit(solution)/shard_map/ppermute | solution.py:80
  30.1 11.5 %collective-permute-start.8 = (bf16[2,192,256]{2,1,0:T(8,128)(2,1)S(1)}, bf16[2,192,256]{2,1,0:T(8,128)(2,1)S(1)}, u32[]{:S(2)}, u32[]{:S(2)}) collective-permute-start(bf16[2,192,256]{2,1,0:T(8,128)(2,1)S(1)} %maximum_select_fusion.4), channel_id=1, source_target_pairs={{0,24},{24,0},{1,25},{25,1},{2,26},{26,2},{3,27},{27,3},{4,28},{28... | collective-permute-start | bytes 589832 | tf_op jit(solution)/shard_map/ppermute | solution.py:21
  38.5 28.7 %collective-permute-start.3 = (bf16[2,3,192,256]{3,2,1,0:T(8,128)(2,1)S(1)}, bf16[2,3,192,256]{3,2,1,0:T(8,128)(2,1)S(1)}, u32[]{:S(2)}, u32[]{:S(2)}) collective-permute-start(bf16[2,3,192,256]{3,2,1,0:T(8,128)(2,1)S(1)} %pad_maximum_fusion.refs_0_), channel_id=1, source_target_pairs={{0,6},{6,12},{12,18},{18,0},{1,7},{7,13},{13,19},{19,1},{2,8},{8,1... | collective-permute-start | bytes 1769480 | tf_op jit(solution)/shard_map/ppermute | solution.py:21
  41.7 14.8 %collective-permute-start.10 = (bf16[768,256]{1,0:T(8,128)(2,1)S(1)}, bf16[768,256]{1,0:T(8,128)(2,1)S(1)}, u32[]{:S(2)}, u32[]{:S(2)}) collective-permute-start(bf16[768,256]{1,0:T(8,128)(2,1)S(1)} %bitcast.27), channel_id=1, source_target_pairs={{0,192},{24,600},{96,288},{120,696},{192,384},{216,24},{288,480},{... | collective-permute-start | bytes 1179656 | tf_op jit(solution)/shard_map/ppermute | solution.py:28
  47.5 16.9 %collective-permute-start.9 = (bf16[768,256]{1,0:T(8,128)(2,1)S(1)}, bf16[768,256]{1,0:T(8,128)(2,1)S(1)}, u32[]{:S(2)}, u32[]{:S(2)}) collective-permute-start(bf16[768,256]{1,0:T(8,128)(2,1)S(1)} %bitcast.28), channel_id=1, source_target_pairs={{0,96},{24,696},{96,192},{120,24},{192,288},{216,120},{288,384},{3... | collective-permute-start | bytes 1179656 | tf_op jit(solution)/shard_map/ppermute | solution.py:28
  50.5 22.1 %collective-permute-start.4 = (bf16[2,3,192,256]{3,2,1,0:T(8,128)(2,1)S(1)}, bf16[2,3,192,256]{3,2,1,0:T(8,128)(2,1)S(1)}, u32[]{:S(2)}, u32[]{:S(2)}) collective-permute-start(bf16[2,3,192,256]{3,2,1,0:T(8,128)(2,1)S(1)} %pad_maximum_fusion.refs_0_), channel_id=1, source_target_pairs={{0,18},{6,0},{12,6},{18,12},{1,19},{7,1},{13,7},{19,13},{2,20},{8,... | collective-permute-start | bytes 1769480 | tf_op jit(solution)/shard_map/ppermute | solution.py:21
  56.5 23.0 %collective-permute-start.11 = (bf16[768,256]{1,0:T(8,128)(2,1)S(1)}, bf16[768,256]{1,0:T(8,128)(2,1)S(1)}, u32[]{:S(2)}, u32[]{:S(2)}) collective-permute-start(bf16[768,256]{1,0:T(8,128)(2,1)S(1)} %collective-permute-done.10.refs_7_), channel_id=1, source_target_pairs={{0,96},{24,696},{96,192},{120,24},{192,288},{216,120},{288,384},{3... | collective-permute-start | bytes 1179656 | tf_op jit(solution)/shard_map/ppermute | solution.py:28
  60.7 8.9 %collective-permute-start.12 = (bf16[384,256]{1,0:T(8,128)(2,1)S(1)}, bf16[384,256]{1,0:T(8,128)(2,1)S(1)}, u32[]{:S(2)}, u32[]{:S(2)}) collective-permute-start(bf16[384,256]{1,0:T(8,128)(2,1)S(1)} %constant_dynamic-slice_fusion.4), channel_id=1, source_target_pairs={{0,192},{24,600},{96,288},{120,696},{192,384},{216,24},{288,480},{... | collective-permute-start | bytes 589832 | tf_op jit(solution)/shard_map/ppermute | solution.py:28
  64.5 20.3 %collective-permute-start.14 = (bf16[768,256]{1,0:T(8,128)(2,1)S(1)}, bf16[768,256]{1,0:T(8,128)(2,1)S(1)}, u32[]{:S(2)}, u32[]{:S(2)}) collective-permute-start(bf16[768,256]{1,0:T(8,128)(2,1)S(1)} %collective-permute-done.10.refs_7_), channel_id=1, source_target_pairs={{0,24},{24,0},{1,25},{25,1},{2,26},{26,2},{3,27},{27,3},{4,28},{28... | collective-permute-start | bytes 1179656 | tf_op jit(solution)/shard_map/ppermute | solution.py:21
  67.2 17.6 %collective-permute-start.13 = (bf16[768,256]{1,0:T(8,128)(2,1)S(1)}, bf16[768,256]{1,0:T(8,128)(2,1)S(1)}, u32[]{:S(2)}, u32[]{:S(2)}) collective-permute-start(bf16[768,256]{1,0:T(8,128)(2,1)S(1)} %collective-permute-done.9.refs_6_), channel_id=1, source_target_pairs={{0,24},{24,0},{1,25},{25,1},{2,26},{26,2},{3,27},{27,3},{4,28},{28... | collective-permute-start | bytes 1179656 | tf_op jit(solution)/shard_map/ppermute | solution.py:21
  69.6 15.2 %collective-permute-start.5 = (bf16[3,192,256]{2,1,0:T(8,128)(2,1)S(1)}, bf16[3,192,256]{2,1,0:T(8,128)(2,1)S(1)}, u32[]{:S(2)}, u32[]{:S(2)}) collective-permute-start(bf16[3,192,256]{2,1,0:T(8,128)(2,1)S(1)} %slice_bitcast_fusion.1), channel_id=1, source_target_pairs={{0,6},{6,12},{12,18},{18,0},{1,7},{7,13},{13,19},{19,1},{2,8},{8,1... | collective-permute-start | bytes 884744 | tf_op jit(solution)/shard_map/ppermute | solution.py:21
  72.7 8.7 %collective-permute-start.16 = (bf16[384,256]{1,0:T(8,128)(2,1)S(1)}, bf16[384,256]{1,0:T(8,128)(2,1)S(1)}, u32[]{:S(2)}, u32[]{:S(2)}) collective-permute-start(bf16[384,256]{1,0:T(8,128)(2,1)S(1)} %collective-permute-done.12.refs_9_), channel_id=1, source_target_pairs={{0,24},{24,0},{1,25},{25,1},{2,26},{26,2},{3,27},{27,3},{4,28},{28... | collective-permute-start | bytes 589832 | tf_op jit(solution)/shard_map/ppermute | solution.py:21
  79.4 11.9 %collective-permute-start.15 = (bf16[768,256]{1,0:T(8,128)(2,1)S(1)}, bf16[768,256]{1,0:T(8,128)(2,1)S(1)}, u32[]{:S(2)}, u32[]{:S(2)}) collective-permute-start(bf16[768,256]{1,0:T(8,128)(2,1)S(1)} %collective-permute-done.11.refs_8_), channel_id=1, source_target_pairs={{0,24},{24,0},{1,25},{25,1},{2,26},{26,2},{3,27},{27,3},{4,28},{28... | collective-permute-start | bytes 1179656 | tf_op jit(solution)/shard_map/ppermute | solution.py:21
  81.4 10.0 %collective-permute-start.6 = (bf16[3,192,256]{2,1,0:T(8,128)(2,1)S(1)}, bf16[3,192,256]{2,1,0:T(8,128)(2,1)S(1)}, u32[]{:S(2)}, u32[]{:S(2)}) collective-permute-start(bf16[3,192,256]{2,1,0:T(8,128)(2,1)S(1)} %slice_bitcast_fusion), channel_id=1, source_target_pairs={{0,18},{6,0},{12,6},{18,12},{1,19},{7,1},{13,7},{19,13},{2,20},{8,... | collective-permute-start | bytes 884744 | tf_op jit(solution)/shard_map/ppermute | solution.py:21
  93.4 40.7 %copy-start = (bf16[6144,128]{1,0:T(8,128)(2,1)S(1)}, bf16[6144,128]{1,0:T(8,128)(2,1)}, u32[]{:S(2)}) copy-start(bf16[6144,128]{1,0:T(8,128)(2,1)} %param.5) | copy-start | bytes 4718596
  124.3 37.9 %all-to-all-start.1 = ((bf16[24,8,1536]{2,1,0:T(8,128)(2,1)}), bf16[24,8,1536]{2,1,0:T(8,128)(2,1)S(1)}, u32[]{:S(2)}, u32[]{:S(2)}) async-start(bf16[24,8,1536]{2,1,0:T(8,128)(2,1)} %bitcast.17), calls=%async_computation.1 | async-start | bytes 1179648 | tf_op jit(solution)/shard_map/all_to_all | solution.py:32
  134.2 17.4 %collective-permute-start.17 = (bf16[1536,128]{1,0:T(8,128)(2,1)S(1)}, bf16[1536,128]{1,0:T(8,128)(2,1)S(1)}, u32[]{:S(2)}, u32[]{:S(2)}) collective-permute-start(bf16[1536,128]{1,0:T(8,128)(2,1)S(1)} %get-tuple-element.7), channel_id=1, source_target_pairs={{0,6},{6,12},{12,18},{18,0},{1,7},{7,13},{13,19},{19,1},{2,8},{8,1... | collective-permute-start | bytes 1179656 | tf_op jit(solution)/shard_map/ppermute | solution.py:21
  137.4 24.2 %collective-permute-start.18 = (bf16[1536,128]{1,0:T(8,128)(2,1)S(1)}, bf16[1536,128]{1,0:T(8,128)(2,1)S(1)}, u32[]{:S(2)}, u32[]{:S(2)}) collective-permute-start(bf16[1536,128]{1,0:T(8,128)(2,1)S(1)} %get-tuple-element.9), channel_id=1, source_target_pairs={{0,12},{6,18},{12,0},{18,6},{1,13},{7,19},{13,1},{19,7},{2,14},{8,... | collective-permute-start | bytes 1179656 | tf_op jit(solution)/shard_map/ppermute | solution.py:21
  141.7 20.5 %collective-permute-start.19 = (bf16[1536,128]{1,0:T(8,128)(2,1)S(1)}, bf16[1536,128]{1,0:T(8,128)(2,1)S(1)}, u32[]{:S(2)}, u32[]{:S(2)}) collective-permute-start(bf16[1536,128]{1,0:T(8,128)(2,1)S(1)} %get-tuple-element.6), channel_id=1, source_target_pairs={{0,18},{6,0},{12,6},{18,12},{1,19},{7,1},{13,7},{19,13},{2,20},{8,... | collective-permute-start | bytes 1179656 | tf_op jit(solution)/shard_map/ppermute | solution.py:21

commit v4 on v2

--- a/solution.py
+++ b/solution.py
@@ -58,14 +58,25 @@
     total += jnp.dot(a[:, :half], low, preferred_element_type=F32)
     total += jnp.dot(a[:, half:], high, preferred_element_type=F32)
     w_ref[...] = total
-    wt_ref[...] = total.T.reshape(wt_ref.shape).astype(BF16)
+    turned = total.T.reshape((NY, NZH, NCO) + wt_ref.shape[3:])
+    for zh in range(NZH):
+        for c in range(NCO):
+            wt_ref[:, c, zh] = turned[:, zh, c].astype(BF16)
 
 
 def second_kernel(w_ref, *refs):
     s_ref = refs[-1]
     x = lax.axis_index("x")
+    run = w_ref.shape[2] // 2
     for s in range(NX):
-        s_ref[lax.rem(x + (NX - s), NX)] = jnp.dot(w_ref[...], refs[s][...], preferred_element_type=F32)
+        total = jnp.zeros(s_ref.shape[1:], F32)
+        for zh in range(NZH):
+            for pair in range(2):
+                rows = pl.ds((pair * NZH + zh) * run, run)
+                total += jnp.dot(
+                    w_ref[zh, :, pair * run : (pair + 1) * run], refs[s][rows], preferred_element_type=F32
+                )
+        s_ref[lax.rem(x + (NX - s), NX)] = total
 
 
 def whole(amplitudes, integrals, dressing):
@@ -99,7 +110,7 @@
         first_kernel,
         out_shape=(
             jax.ShapeDtypeStruct((rows, wide), F32),
-            jax.ShapeDtypeStruct((wide // 8, 8, rows), BF16),
+            jax.ShapeDtypeStruct((NY, NCO, NZH, wide // (NY * NZH * NCO), rows), BF16),
         ),
         in_specs=[VMEM_SPEC] * 14,
         out_specs=(VMEM_SPEC,) * 2,
@@ -108,14 +119,15 @@
         name="first",
     )(*a, *v)
 
-    wt = exchange(wt, ROW)
-    wt = wt.reshape(NX, 8, 8, rows).transpose(0, 2, 1, 3).reshape(NX, 1, 8, deep)
-    wt = jnp.broadcast_to(wt, (NX, NZL, 8, deep)).reshape(NX * NZL, 8, deep)
-    wt = exchange(wt, COL).reshape(NX * NZL * 8, deep)
+    deal = wt.shape[3]
+    wt = exchange(wt.reshape(NY * NCO, NZH, deal, rows), ("y", "co"))
+    wt = wt.reshape(NX, 4, NZH, deal, rows).transpose(2, 0, 3, 1, 4).reshape(NZH, NX, 1, deal, 4 * rows)
+    wt = jnp.broadcast_to(wt, (NZH, NX, NZL, deal, 4 * rows)).reshape(NZH * NX * NZL, deal, 4 * rows)
+    wt = exchange(wt, ("zh", "x", "zl")).reshape(NZH, NX * NZL * deal, 4 * rows)
 
     part = pl.pallas_call(
         second_kernel,
-        out_shape=jax.ShapeDtypeStruct((NX, NX * NZL * 8, dressing.shape[1]), F32),
+        out_shape=jax.ShapeDtypeStruct((NX, wt.shape[1], dressing.shape[1]), F32),
         in_specs=[VMEM_SPEC] * 5,
         out_specs=VMEM_SPEC,
         compiler_params=pltpu.CompilerParams(vmem_limit_bytes=16 * 2**20),

time: 183 us -> 178 us (0.973)
  blocking collectives: 34.4 us -> 28.1 us
    all_to_all x2, blocking collectives: 34.4 us -> 28.1 us  [exchange(): return lax.all_to_all(value, axis, 0, 0, tiled=True)]
where the time goes in v4:
time: 178 us
  starting transfers between devices  99.8 us (56%)
  waiting for transfers between devices  42.2 us (24%)
  blocking collectives  28.1 us (16%)
  local copies, waits for them, and re-layouts  3.03 us (2%)
  Pallas kernels  2.79 us (2%)
    ppermute x13, starting transfers between devices, permute(): return lax.ppermute(value, axis, shift(n, s))  50.4 us
    ppermute x13, waiting for transfers between devices, permute(): return lax.ppermute(value, axis, shift(n, s))  37.1 us
    all_to_all x2, starting transfers between devices, exchange(): return lax.all_to_all(value, axis, 0, 0, tiled=True)  32.6 us
    all_to_all x2, blocking collectives, exchange(): return lax.all_to_all(value, axis, 0, 0, tiled=True)  28.1 us
    ppermute x4, starting transfers between devices, opposed(): return lax.ppermute(value, ('y', 'co'), pairs)  16.8 us
    ppermute x4, waiting for transfers between devices, opposed(): return lax.ppermute(value, ('y', 'co'), pairs)  5.11 us
  transfers between devices with their start and end apart: 19, of which 9 were waited for; matrix products, arithmetic and copies ran while one was open for 0% of the time, Pallas kernels for 0%

profile of v4, /device:TPU:1, one launch (start us, length us, event | category | flops | bytes accessed | tf_op | source)
XLA Modules:
  0.0 177.6 jit_solution(5714837426703234338)
XLA Ops:
  0.6 0.0 copy-start.1
  0.6 1.8 %broadcast_in_dim.6 = bf16[6,192,256]{2,1,0:T(8,128)(2,1)} broadcast(bf16[192,256]{1,0:T(8,128)(2,1)} %param.3), dimensions={1,2} | broadcast | bytes 688128 | tf_op jit(solution)/shard_map/broadcast_in_dim | solution.py:87
  2.4 12.6 %all-to-all-start = ((bf16[6,192,256]{2,1,0:T(8,128)(2,1)}), bf16[6,192,256]{2,1,0:T(8,128)(2,1)S(1)}, u32[]{:S(2)}, u32[]{:S(2)}) async-start(bf16[6,192,256]{2,1,0:T(8,128)(2,1)} %broadcast_in_dim.6), calls=%async_computation | async-start | bytes 1179648 | tf_op jit(solution)/shard_map/all_to_all | solution.py:32
  15.0 0.0 copy-done.1
  15.1 9.7 %collective-permute-start.4 = (bf16[192,256]{1,0:T(8,128)(2,1)S(1)}, bf16[192,256]{1,0:T(8,128)(2,1)S(1)}, u32[]{:S(2)}, u32[]{:S(2)}) collective-permute-start(bf16[192,256]{1,0:T(8,128)(2,1)S(1)} %copy-done.1), channel_id=1, source_target_pairs={{0,48},{48,0},{1,49},{49,1},{2,50},{50,2},{3,51},{51,3},{4,52},{52... | collective-permute-start | bytes 294920 | tf_op jit(solution)/shard_map/ppermute | solution.py:21
  24.8 11.5 %collective-permute-done.4 = bf16[192,256]{1,0:T(8,128)(2,1)S(1)} collective-permute-done((bf16[192,256]{1,0:T(8,128)(2,1)S(1)}, bf16[192,256]{1,0:T(8,128)(2,1)S(1)}, u32[]{:S(2)}, u32[]{:S(2)}) %collective-permute-start.4) | collective-permute-done | bytes 98336 | tf_op jit(solution)/shard_map/ppermute | solution.py:21
  36.4 4.6 %collective-permute-start.5 = (bf16[2,192,256]{2,1,0:T(8,128)(2,1)S(1)}, bf16[2,192,256]{2,1,0:T(8,128)(2,1)S(1)}, u32[]{:S(2)}, u32[]{:S(2)}) collective-permute-start(bf16[2,192,256]{2,1,0:T(8,128)(2,1)S(1)} %maximum_select_fusion.2), channel_id=1, source_target_pairs={{0,24},{24,0},{1,25},{25,1},{2,26},{26,2},{3,27},{27,3},{4,28},{28... | collective-permute-start | bytes 589832 | tf_op jit(solution)/shard_map/ppermute | solution.py:21
  41.0 1.0 collective-permute-done.5
  42.1 5.9 %collective-permute-start.7 = (bf16[768,256]{1,0:T(8,128)(2,1)S(1)}, bf16[768,256]{1,0:T(8,128)(2,1)S(1)}, u32[]{:S(2)}, u32[]{:S(2)}) collective-permute-start(bf16[768,256]{1,0:T(8,128)(2,1)S(1)} %bitcast.21), channel_id=1, source_target_pairs={{0,192},{24,600},{96,288},{120,696},{192,384},{216,24},{288,480},{... | collective-permute-start | bytes 1179656 | tf_op jit(solution)/shard_map/ppermute | solution.py:28
  48.0 0.0 all-to-all-done
  48.0 3.1 %collective-permute-start = (bf16[2,3,192,256]{3,2,1,0:T(8,128)(2,1)S(1)}, bf16[2,3,192,256]{3,2,1,0:T(8,128)(2,1)S(1)}, u32[]{:S(2)}, u32[]{:S(2)}) collective-permute-start(bf16[2,3,192,256]{3,2,1,0:T(8,128)(2,1)S(1)} %bitcast.18), channel_id=1, source_target_pairs={{0,6},{6,12},{12,18},{18,0},{1,7},{7,13},{13,19},{19,1},{2,8},{8,1... | collective-permute-start | bytes 1769480 | tf_op jit(solution)/shard_map/ppermute | solution.py:21
  51.1 3.0 %collective-permute-start.6 = (bf16[768,256]{1,0:T(8,128)(2,1)S(1)}, bf16[768,256]{1,0:T(8,128)(2,1)S(1)}, u32[]{:S(2)}, u32[]{:S(2)}) collective-permute-start(bf16[768,256]{1,0:T(8,128)(2,1)S(1)} %bitcast.22), channel_id=1, source_target_pairs={{0,96},{24,696},{96,192},{120,24},{192,288},{216,120},{288,384},{3... | collective-permute-start | bytes 1179656 | tf_op jit(solution)/shard_map/ppermute | solution.py:28
  54.1 2.8 %collective-permute-done.7.refs_7_ = bf16[768,256]{1,0:T(8,128)(2,1)S(1)} collective-permute-done((bf16[768,256]{1,0:T(8,128)(2,1)S(1)}, bf16[768,256]{1,0:T(8,128)(2,1)S(1)}, u32[]{:S(2)}, u32[]{:S(2)}) %collective-permute-start.7) | collective-permute-done | bytes 393248 | tf_op jit(solution)/shard_map/ppermute | solution.py:28
  56.9 4.2 %collective-permute-start.8 = (bf16[768,256]{1,0:T(8,128)(2,1)S(1)}, bf16[768,256]{1,0:T(8,128)(2,1)S(1)}, u32[]{:S(2)}, u32[]{:S(2)}) collective-permute-start(bf16[768,256]{1,0:T(8,128)(2,1)S(1)} %collective-permute-done.7.refs_7_), channel_id=1, source_target_pairs={{0,96},{24,696},{96,192},{120,24},{192,288},{216,120},{288,384},{3... | collective-permute-start | bytes 1179656 | tf_op jit(solution)/shard_map/ppermute | solution.py:28
  61.1 4.4 %collective-permute-start.1 = (bf16[2,3,192,256]{3,2,1,0:T(8,128)(2,1)S(1)}, bf16[2,3,192,256]{3,2,1,0:T(8,128)(2,1)S(1)}, u32[]{:S(2)}, u32[]{:S(2)}) collective-permute-start(bf16[2,3,192,256]{3,2,1,0:T(8,128)(2,1)S(1)} %bitcast.19), channel_id=1, source_target_pairs={{0,18},{6,0},{12,6},{18,12},{1,19},{7,1},{13,7},{19,13},{2,20},{8,... | collective-permute-start | bytes 1769480 | tf_op jit(solution)/shard_map/ppermute | solution.py:21
  65.5 3.7 %collective-permute-start.9 = (bf16[384,256]{1,0:T(8,128)(2,1)S(1)}, bf16[384,256]{1,0:T(8,128)(2,1)S(1)}, u32[]{:S(2)}, u32[]{:S(2)}) collective-permute-start(bf16[384,256]{1,0:T(8,128)(2,1)S(1)} %constant_dynamic-slice_fusion.4), channel_id=1, source_target_pairs={{0,192},{24,600},{96,288},{120,696},{192,384},{216,24},{288,480},{... | collective-permute-start | bytes 589832 | tf_op jit(solution)/shard_map/ppermute | solution.py:28
  69.3 0.0 collective-permute-done.6.refs_6_
  69.3 2.6 %collective-permute-start.11 = (bf16[768,256]{1,0:T(8,128)(2,1)S(1)}, bf16[768,256]{1,0:T(8,128)(2,1)S(1)}, u32[]{:S(2)}, u32[]{:S(2)}) collective-permute-start(bf16[768,256]{1,0:T(8,128)(2,1)S(1)} %collective-permute-done.7.refs_7_), channel_id=1, source_target_pairs={{0,24},{24,0},{1,25},{25,1},{2,26},{26,2},{3,27},{27,3},{4,28},{28... | collective-permute-start | bytes 1179656 | tf_op jit(solution)/shard_map/ppermute | solution.py:21
  71.9 2.3 %collective-permute-done.9.refs_9_ = bf16[384,256]{1,0:T(8,128)(2,1)S(1)} collective-permute-done((bf16[384,256]{1,0:T(8,128)(2,1)S(1)}, bf16[384,256]{1,0:T(8,128)(2,1)S(1)}, u32[]{:S(2)}, u32[]{:S(2)}) %collective-permute-start.9) | collective-permute-done | bytes 196640 | tf_op jit(solution)/shard_map/ppermute | solution.py:28
  74.2 4.7 %collective-permute-start.10 = (bf16[768,256]{1,0:T(8,128)(2,1)S(1)}, bf16[768,256]{1,0:T(8,128)(2,1)S(1)}, u32[]{:S(2)}, u32[]{:S(2)}) collective-permute-start(bf16[768,256]{1,0:T(8,128)(2,1)S(1)} %collective-permute-done.6.refs_6_), channel_id=1, source_target_pairs={{0,24},{24,0},{1,25},{25,1},{2,26},{26,2},{3,27},{27,3},{4,28},{28... | collective-permute-start | bytes 1179656 | tf_op jit(solution)/shard_map/ppermute | solution.py:21
  78.9 0.0 collective-permute-done.8.refs_8_
  78.9 1.9 %collective-permute-start.13 = (bf16[384,256]{1,0:T(8,128)(2,1)S(1)}, bf16[384,256]{1,0:T(8,128)(2,1)S(1)}, u32[]{:S(2)}, u32[]{:S(2)}) collective-permute-start(bf16[384,256]{1,0:T(8,128)(2,1)S(1)} %collective-permute-done.9.refs_9_), channel_id=1, source_target_pairs={{0,24},{24,0},{1,25},{25,1},{2,26},{26,2},{3,27},{27,3},{4,28},{28... | collective-permute-start | bytes 589832 | tf_op jit(solution)/shard_map/ppermute | solution.py:21
  80.8 0.0 collective-permute-done.refs_1_
  80.8 2.4 %collective-permute-start.12 = (bf16[768,256]{1,0:T(8,128)(2,1)S(1)}, bf16[768,256]{1,0:T(8,128)(2,1)S(1)}, u32[]{:S(2)}, u32[]{:S(2)}) collective-permute-start(bf16[768,256]{1,0:T(8,128)(2,1)S(1)} %collective-permute-done.8.refs_8_), channel_id=1, source_target_pairs={{0,24},{24,0},{1,25},{25,1},{2,26},{26,2},{3,27},{27,3},{4,28},{28... | collective-permute-start | bytes 1179656 | tf_op jit(solution)/shard_map/ppermute | solution.py:21
  83.3 0.0 collective-permute-done.1.refs_2_
  83.3 1.9 %collective-permute-start.2 = (bf16[3,192,256]{2,1,0:T(8,128)(2,1)S(1)}, bf16[3,192,256]{2,1,0:T(8,128)(2,1)S(1)}, u32[]{:S(2)}, u32[]{:S(2)}) collective-permute-start(bf16[3,192,256]{2,1,0:T(8,128)(2,1)S(1)} %slice_bitcast_fusion.1), channel_id=1, source_target_pairs={{0,6},{6,12},{12,18},{18,0},{1,7},{7,13},{13,19},{19,1},{2,8},{8,1... | collective-permute-start | bytes 884744 | tf_op jit(solution)/shard_map/ppermute | solution.py:21
  85.3 0.0 collective-permute-done.13.refs_13_
  85.3 4.6 %collective-permute-start.3 = (bf16[3,192,256]{2,1,0:T(8,128)(2,1)S(1)}, bf16[3,192,256]{2,1,0:T(8,128)(2,1)S(1)}, u32[]{:S(2)}, u32[]{:S(2)}) collective-permute-start(bf16[3,192,256]{2,1,0:T(8,128)(2,1)S(1)} %slice_bitcast_fusion), channel_id=1, source_target_pairs={{0,18},{6,0},{12,6},{18,12},{1,19},{7,1},{13,7},{19,13},{2,20},{8,... | collective-permute-start | bytes 884744 | tf_op jit(solution)/shard_map/ppermute | solution.py:21
  89.9 0.0 collective-permute-done.11.refs_11_
  89.9 0.0 collective-permute-done.10.refs_10_
  89.9 0.0 collective-permute-done.12.refs_12_
  89.9 5.1 %collective-permute-done.2.refs_3_ = bf16[3,192,256]{2,1,0:T(8,128)(2,1)S(1)} collective-permute-done((bf16[3,192,256]{2,1,0:T(8,128)(2,1)S(1)}, bf16[3,192,256]{2,1,0:T(8,128)(2,1)S(1)}, u32[]{:S(2)}, u32[]{:S(2)}) %collective-permute-start.2) | collective-permute-done | bytes 294944 | tf_op jit(solution)/shard_map/ppermute | solution.py:21
  95.0 0.9 collective-permute-done.3.refs_4_
  95.9 2.0 %first.1 = (f32[192,256]{1,0:T(8,128)}, bf16[8,2,2,8,192]{4,3,2,1,0:T(8,128)(2,1)S(1)}) custom-call(bf16[2,3,192,256]{3,2,1,0:T(8,128)(2,1)S(1)} %bitcast.20, bf16[2,3,192,256]{3,2,1,0:T(8,128)(2,1)S(1)} %collective-permute-done.refs_1_, bf16[2,3,192,256]{3,2,1,0:T(8,128)(2,1)S(1)} %collective-permute-done.1.refs_2_, ...), custom_call_target="tpu_custom_call" | custom-call | tf_op jit(solution)/shard_map/first/pallas_call | solution.py:109
  97.9 0.0 copy-start
  97.9 17.0 %all_to_all.20 = bf16[16,2,8,192]{3,2,1,0:T(8,128)(2,1)S(1)} all-to-all(bf16[16,2,8,192]{3,2,1,0:T(8,128)(2,1)S(1)} %bitcast.24), channel_id=1, replica_groups=mesh['y'=8,'zh'=2,'co'=2,'x'=4,'zl'=6] {'y','co'}, dimensions={0} | all-to-all | bytes 196608 | tf_op jit(solution)/shard_map/all_to_all | solution.py:32
  115.0 0.1 copy.5
  115.0 0.1 broadcast_in_dim.14
  115.2 0.9 broadcast_in_dim.15
  116.0 19.9 %all-to-all-start.2 = ((bf16[48,8,768]{2,1,0:T(8,128)(2,1)}), bf16[48,8,768]{2,1,0:T(8,128)(2,1)S(1)}, u32[]{:S(2)}, u32[]{:S(2)}) async-start(bf16[48,8,768]{2,1,0:T(8,128)(2,1)} %bitcast.12), calls=%async_computation.2 | async-start | bytes 1179648 | tf_op jit(solution)/shard_map/all_to_all | solution.py:32
  136.0 0.0 copy-done
  136.0 0.1 constant_dynamic-slice_fusion
  136.1 3.0 %collective-permute-start.14 = (bf16[1536,128]{1,0:T(8,128)(2,1)S(1)}, bf16[1536,128]{1,0:T(8,128)(2,1)S(1)}, u32[]{:S(2)}, u32[]{:S(2)}) collective-permute-start(bf16[1536,128]{1,0:T(8,128)(2,1)S(1)} %get-tuple-element.7), channel_id=1, source_target_pairs={{0,6},{6,12},{12,18},{18,0},{1,7},{7,13},{13,19},{19,1},{2,8},{8,1... | collective-permute-start | bytes 1179656 | tf_op jit(solution)/shard_map/ppermute | solution.py:21
  139.2 4.3 %collective-permute-start.15 = (bf16[1536,128]{1,0:T(8,128)(2,1)S(1)}, bf16[1536,128]{1,0:T(8,128)(2,1)S(1)}, u32[]{:S(2)}, u32[]{:S(2)}) collective-permute-start(bf16[1536,128]{1,0:T(8,128)(2,1)S(1)} %get-tuple-element.9), channel_id=1, source_target_pairs={{0,12},{6,18},{12,0},{18,6},{1,13},{7,19},{13,1},{19,7},{2,14},{8,... | collective-permute-start | bytes 1179656 | tf_op jit(solution)/shard_map/ppermute | solution.py:21
  143.5 3.1 %collective-permute-start.16 = (bf16[1536,128]{1,0:T(8,128)(2,1)S(1)}, bf16[1536,128]{1,0:T(8,128)(2,1)S(1)}, u32[]{:S(2)}, u32[]{:S(2)}) collective-permute-start(bf16[1536,128]{1,0:T(8,128)(2,1)S(1)} %get-tuple-element.6), channel_id=1, source_target_pairs={{0,18},{6,0},{12,6},{18,12},{1,19},{7,1},{13,7},{19,13},{2,20},{8,... | collective-permute-start | bytes 1179656 | tf_op jit(solution)/shard_map/ppermute | solution.py:21
  146.6 6.9 %collective-permute-done.14.refs_1_ = bf16[1536,128]{1,0:T(8,128)(2,1)S(1)} collective-permute-done((bf16[1536,128]{1,0:T(8,128)(2,1)S(1)}, bf16[1536,128]{1,0:T(8,128)(2,1)S(1)}, u32[]{:S(2)}, u32[]{:S(2)}) %collective-permute-start.14) | collective-permute-done | bytes 393248 | tf_op jit(solution)/shard_map/ppermute | solution.py:21
  153.5 11.2 %collective-permute-done.15.refs_2_ = bf16[1536,128]{1,0:T(8,128)(2,1)S(1)} collective-permute-done((bf16[1536,128]{1,0:T(8,128)(2,1)S(1)}, bf16[1536,128]{1,0:T(8,128)(2,1)S(1)}, u32[]{:S(2)}, u32[]{:S(2)}) %collective-permute-start.15) | collective-permute-done | bytes 393248 | tf_op jit(solution)/shard_map/ppermute | solution.py:21
  164.6 0.4 collective-permute-done.16.refs_3_
  165.1 0.0 all-to-all-done.2
  165.1 0.8 second.1
  165.8 11.1 %all_to_all.21 = f32[4,192,128]{2,1,0:T(8,128)S(1)} all-to-all(f32[4,192,128]{2,1,0:T(8,128)S(1)} %second.1), channel_id=1, replica_groups=mesh['y'=8,'zh'=2,'co'=2,'x'=4,'zl'=6] {'x'}, dimensions={0} | all-to-all | bytes 786432 | tf_op jit(solution)/shard_map/all_to_all | solution.py:32
  177.0 0.7 reduce_sum.9
  (6 shorter events, 0.1 us)
Async XLA Ops:
  0.6 14.4 %copy-start.1 = (bf16[192,256]{1,0:T(8,128)(2,1)S(1)}, bf16[192,256]{1,0:T(8,128)(2,1)}, u32[]{:S(2)}) copy-start(bf16[192,256]{1,0:T(8,128)(2,1)} %param.4) | copy-start | bytes 294916
  2.4 45.6 %all-to-all-start = ((bf16[6,192,256]{2,1,0:T(8,128)(2,1)}), bf16[6,192,256]{2,1,0:T(8,128)(2,1)S(1)}, u32[]{:S(2)}, u32[]{:S(2)}) async-start(bf16[6,192,256]{2,1,0:T(8,128)(2,1)} %broadcast_in_dim.6), calls=%async_computation | async-start | bytes 1179648 | tf_op jit(solution)/shard_map/all_to_all | solution.py:32
  15.1 21.3 %collective-permute-start.4 = (bf16[192,256]{1,0:T(8,128)(2,1)S(1)}, bf16[192,256]{1,0:T(8,128)(2,1)S(1)}, u32[]{:S(2)}, u32[]{:S(2)}) collective-permute-start(bf16[192,256]{1,0:T(8,128)(2,1)S(1)} %copy-done.1), channel_id=1, source_target_pairs={{0,48},{48,0},{1,49},{49,1},{2,50},{50,2},{3,51},{51,3},{4,52},{52... | collective-permute-start | bytes 294920 | tf_op jit(solution)/shard_map/ppermute | solution.py:21
  36.4 5.7 %collective-permute-start.5 = (bf16[2,192,256]{2,1,0:T(8,128)(2,1)S(1)}, bf16[2,192,256]{2,1,0:T(8,128)(2,1)S(1)}, u32[]{:S(2)}, u32[]{:S(2)}) collective-permute-start(bf16[2,192,256]{2,1,0:T(8,128)(2,1)S(1)} %maximum_select_fusion.2), channel_id=1, source_target_pairs={{0,24},{24,0},{1,25},{25,1},{2,26},{26,2},{3,27},{27,3},{4,28},{28... | collective-permute-start | bytes 589832 | tf_op jit(solution)/shard_map/ppermute | solution.py:21
  42.1 14.8 %collective-permute-start.7 = (bf16[768,256]{1,0:T(8,128)(2,1)S(1)}, bf16[768,256]{1,0:T(8,128)(2,1)S(1)}, u32[]{:S(2)}, u32[]{:S(2)}) collective-permute-start(bf16[768,256]{1,0:T(8,128)(2,1)S(1)} %bitcast.21), channel_id=1, source_target_pairs={{0,192},{24,600},{96,288},{120,696},{192,384},{216,24},{288,480},{... | collective-permute-start | bytes 1179656 | tf_op jit(solution)/shard_map/ppermute | solution.py:28
  48.0 32.8 %collective-permute-start = (bf16[2,3,192,256]{3,2,1,0:T(8,128)(2,1)S(1)}, bf16[2,3,192,256]{3,2,1,0:T(8,128)(2,1)S(1)}, u32[]{:S(2)}, u32[]{:S(2)}) collective-permute-start(bf16[2,3,192,256]{3,2,1,0:T(8,128)(2,1)S(1)} %bitcast.18), channel_id=1, source_target_pairs={{0,6},{6,12},{12,18},{18,0},{1,7},{7,13},{13,19},{19,1},{2,8},{8,1... | collective-permute-start | bytes 1769480 | tf_op jit(solution)/shard_map/ppermute | solution.py:21
  51.1 18.2 %collective-permute-start.6 = (bf16[768,256]{1,0:T(8,128)(2,1)S(1)}, bf16[768,256]{1,0:T(8,128)(2,1)S(1)}, u32[]{:S(2)}, u32[]{:S(2)}) collective-permute-start(bf16[768,256]{1,0:T(8,128)(2,1)S(1)} %bitcast.22), channel_id=1, source_target_pairs={{0,96},{24,696},{96,192},{120,24},{192,288},{216,120},{288,384},{3... | collective-permute-start | bytes 1179656 | tf_op jit(solution)/shard_map/ppermute | solution.py:28
  56.9 22.0 %collective-permute-start.8 = (bf16[768,256]{1,0:T(8,128)(2,1)S(1)}, bf16[768,256]{1,0:T(8,128)(2,1)S(1)}, u32[]{:S(2)}, u32[]{:S(2)}) collective-permute-start(bf16[768,256]{1,0:T(8,128)(2,1)S(1)} %collective-permute-done.7.refs_7_), channel_id=1, source_target_pairs={{0,96},{24,696},{96,192},{120,24},{192,288},{216,120},{288,384},{3... | collective-permute-start | bytes 1179656 | tf_op jit(solution)/shard_map/ppermute | solution.py:28
  61.1 22.2 %collective-permute-start.1 = (bf16[2,3,192,256]{3,2,1,0:T(8,128)(2,1)S(1)}, bf16[2,3,192,256]{3,2,1,0:T(8,128)(2,1)S(1)}, u32[]{:S(2)}, u32[]{:S(2)}) collective-permute-start(bf16[2,3,192,256]{3,2,1,0:T(8,128)(2,1)S(1)} %bitcast.19), channel_id=1, source_target_pairs={{0,18},{6,0},{12,6},{18,12},{1,19},{7,1},{13,7},{19,13},{2,20},{8,... | collective-permute-start | bytes 1769480 | tf_op jit(solution)/shard_map/ppermute | solution.py:21
  65.5 8.6 %collective-permute-start.9 = (bf16[384,256]{1,0:T(8,128)(2,1)S(1)}, bf16[384,256]{1,0:T(8,128)(2,1)S(1)}, u32[]{:S(2)}, u32[]{:S(2)}) collective-permute-start(bf16[384,256]{1,0:T(8,128)(2,1)S(1)} %constant_dynamic-slice_fusion.4), channel_id=1, source_target_pairs={{0,192},{24,600},{96,288},{120,696},{192,384},{216,24},{288,480},{... | collective-permute-start | bytes 589832 | tf_op jit(solution)/shard_map/ppermute | solution.py:28
  69.3 20.6 %collective-permute-start.11 = (bf16[768,256]{1,0:T(8,128)(2,1)S(1)}, bf16[768,256]{1,0:T(8,128)(2,1)S(1)}, u32[]{:S(2)}, u32[]{:S(2)}) collective-permute-start(bf16[768,256]{1,0:T(8,128)(2,1)S(1)} %collective-permute-done.7.refs_7_), channel_id=1, source_target_pairs={{0,24},{24,0},{1,25},{25,1},{2,26},{26,2},{3,27},{27,3},{4,28},{28... | collective-permute-start | bytes 1179656 | tf_op jit(solution)/shard_map/ppermute | solution.py:21
  74.2 15.7 %collective-permute-start.10 = (bf16[768,256]{1,0:T(8,128)(2,1)S(1)}, bf16[768,256]{1,0:T(8,128)(2,1)S(1)}, u32[]{:S(2)}, u32[]{:S(2)}) collective-permute-start(bf16[768,256]{1,0:T(8,128)(2,1)S(1)} %collective-permute-done.6.refs_6_), channel_id=1, source_target_pairs={{0,24},{24,0},{1,25},{25,1},{2,26},{26,2},{3,27},{27,3},{4,28},{28... | collective-permute-start | bytes 1179656 | tf_op jit(solution)/shard_map/ppermute | solution.py:21
  78.9 6.4 %collective-permute-start.13 = (bf16[384,256]{1,0:T(8,128)(2,1)S(1)}, bf16[384,256]{1,0:T(8,128)(2,1)S(1)}, u32[]{:S(2)}, u32[]{:S(2)}) collective-permute-start(bf16[384,256]{1,0:T(8,128)(2,1)S(1)} %collective-permute-done.9.refs_9_), channel_id=1, source_target_pairs={{0,24},{24,0},{1,25},{25,1},{2,26},{26,2},{3,27},{27,3},{4,28},{28... | collective-permute-start | bytes 589832 | tf_op jit(solution)/shard_map/ppermute | solution.py:21
  80.8 9.0 %collective-permute-start.12 = (bf16[768,256]{1,0:T(8,128)(2,1)S(1)}, bf16[768,256]{1,0:T(8,128)(2,1)S(1)}, u32[]{:S(2)}, u32[]{:S(2)}) collective-permute-start(bf16[768,256]{1,0:T(8,128)(2,1)S(1)} %collective-permute-done.8.refs_8_), channel_id=1, source_target_pairs={{0,24},{24,0},{1,25},{25,1},{2,26},{26,2},{3,27},{27,3},{4,28},{28... | collective-permute-start | bytes 1179656 | tf_op jit(solution)/shard_map/ppermute | solution.py:21
  83.3 11.7 %collective-permute-start.2 = (bf16[3,192,256]{2,1,0:T(8,128)(2,1)S(1)}, bf16[3,192,256]{2,1,0:T(8,128)(2,1)S(1)}, u32[]{:S(2)}, u32[]{:S(2)}) collective-permute-start(bf16[3,192,256]{2,1,0:T(8,128)(2,1)S(1)} %slice_bitcast_fusion.1), channel_id=1, source_target_pairs={{0,6},{6,12},{12,18},{18,0},{1,7},{7,13},{13,19},{19,1},{2,8},{8,1... | collective-permute-start | bytes 884744 | tf_op jit(solution)/shard_map/ppermute | solution.py:21
  85.3 10.6 %collective-permute-start.3 = (bf16[3,192,256]{2,1,0:T(8,128)(2,1)S(1)}, bf16[3,192,256]{2,1,0:T(8,128)(2,1)S(1)}, u32[]{:S(2)}, u32[]{:S(2)}) collective-permute-start(bf16[3,192,256]{2,1,0:T(8,128)(2,1)S(1)} %slice_bitcast_fusion), channel_id=1, source_target_pairs={{0,18},{6,0},{12,6},{18,12},{1,19},{7,1},{13,7},{19,13},{2,20},{8,... | collective-permute-start | bytes 884744 | tf_op jit(solution)/shard_map/ppermute | solution.py:21
  97.9 38.1 %copy-start = (bf16[6144,128]{1,0:T(8,128)(2,1)S(1)}, bf16[6144,128]{1,0:T(8,128)(2,1)}, u32[]{:S(2)}) copy-start(bf16[6144,128]{1,0:T(8,128)(2,1)} %param.5) | copy-start | bytes 4718596
  116.0 49.0 %all-to-all-start.2 = ((bf16[48,8,768]{2,1,0:T(8,128)(2,1)}), bf16[48,8,768]{2,1,0:T(8,128)(2,1)S(1)}, u32[]{:S(2)}, u32[]{:S(2)}) async-start(bf16[48,8,768]{2,1,0:T(8,128)(2,1)} %bitcast.12), calls=%async_computation.2 | async-start | bytes 1179648 | tf_op jit(solution)/shard_map/all_to_all | solution.py:32
  136.1 17.4 %collective-permute-start.14 = (bf16[1536,128]{1,0:T(8,128)(2,1)S(1)}, bf16[1536,128]{1,0:T(8,128)(2,1)S(1)}, u32[]{:S(2)}, u32[]{:S(2)}) collective-permute-start(bf16[1536,128]{1,0:T(8,128)(2,1)S(1)} %get-tuple-element.7), channel_id=1, source_target_pairs={{0,6},{6,12},{12,18},{18,0},{1,7},{7,13},{13,19},{19,1},{2,8},{8,1... | collective-permute-start | bytes 1179656 | tf_op jit(solution)/shard_map/ppermute | solution.py:21
  139.2 25.5 %collective-permute-start.15 = (bf16[1536,128]{1,0:T(8,128)(2,1)S(1)}, bf16[1536,128]{1,0:T(8,128)(2,1)S(1)}, u32[]{:S(2)}, u32[]{:S(2)}) collective-permute-start(bf16[1536,128]{1,0:T(8,128)(2,1)S(1)} %get-tuple-element.9), channel_id=1, source_target_pairs={{0,12},{6,18},{12,0},{18,6},{1,13},{7,19},{13,1},{19,7},{2,14},{8,... | collective-permute-start | bytes 1179656 | tf_op jit(solution)/shard_map/ppermute | solution.py:21
  143.5 21.6 %collective-permute-start.16 = (bf16[1536,128]{1,0:T(8,128)(2,1)S(1)}, bf16[1536,128]{1,0:T(8,128)(2,1)S(1)}, u32[]{:S(2)}, u32[]{:S(2)}) collective-permute-start(bf16[1536,128]{1,0:T(8,128)(2,1)S(1)} %get-tuple-element.6), channel_id=1, source_target_pairs={{0,18},{6,0},{12,6},{18,12},{1,19},{7,1},{13,7},{19,13},{2,20},{8,... | collective-permute-start | bytes 1179656 | tf_op jit(solution)/shard_map/ppermute | solution.py:21

commit v5 on v4

--- a/solution.py
+++ b/solution.py
@@ -101,10 +101,8 @@
     v = [own, one, two, three, four]
     v += [permute(v[i], "co", NCO, 1) for i in (1, 2, 3, 4)]
 
-    u = [lax.dynamic_slice_in_dim(dressing, x * deep, deep, 0)]
-    for s in (1, 2, 3):
-        piece = lax.dynamic_slice_in_dim(dressing, lax.rem(x + s, NX) * deep, deep, 0)
-        u.append(permute(piece, "x", NX, s))
+    u = [lax.dynamic_slice_in_dim(dressing, lax.rem(x + s, NX) * deep, deep, 0) for s in range(NX)]
+    u = [u[0]] + [permute(u[s], "x", NX, s) for s in (1, 2, 3)]
 
     first_cycle, wt = pl.pallas_call(
         first_kernel,

time: 178 us -> 178 us (level)
  no operation moved by 1% of the time
where the time goes in v5:
time: 178 us
  starting transfers between devices  99.8 us (56%)
  waiting for transfers between devices  42.2 us (24%)
  blocking collectives  28.1 us (16%)
  local copies, waits for them, and re-layouts  3.03 us (2%)
  Pallas kernels  2.78 us (2%)
    ppermute x13, starting transfers between devices, permute(): return lax.ppermute(value, axis, shift(n, s))  50.4 us
    ppermute x13, waiting for transfers between devices, permute(): return lax.ppermute(value, axis, shift(n, s))  37.1 us
    all_to_all x2, starting transfers between devices, exchange(): return lax.all_to_all(value, axis, 0, 0, tiled=True)  32.6 us
    all_to_all x2, blocking collectives, exchange(): return lax.all_to_all(value, axis, 0, 0, tiled=True)  28.1 us
    ppermute x4, starting transfers between devices, opposed(): return lax.ppermute(value, ('y', 'co'), pairs)  16.8 us
    ppermute x4, waiting for transfers between devices, opposed(): return lax.ppermute(value, ('y', 'co'), pairs)  5.11 us
  transfers between devices with their start and end apart: 19, of which 9 were waited for; matrix products, arithmetic and copies ran while one was open for 0% of the time, Pallas kernels for 0%

profile of v5, /device:TPU:1, one launch (start us, length us, event | category | flops | bytes accessed | tf_op | source)
XLA Modules:
  0.0 177.6 jit_solution(4232233347084118903)
XLA Ops:
  0.6 0.0 copy-start.1
  0.6 1.8 %broadcast_in_dim.6 = bf16[6,192,256]{2,1,0:T(8,128)(2,1)} broadcast(bf16[192,256]{1,0:T(8,128)(2,1)} %param.3), dimensions={1,2} | broadcast | bytes 688128 | tf_op jit(solution)/shard_map/broadcast_in_dim | solution.py:87
  2.4 12.6 %all-to-all-start = ((bf16[6,192,256]{2,1,0:T(8,128)(2,1)}), bf16[6,192,256]{2,1,0:T(8,128)(2,1)S(1)}, u32[]{:S(2)}, u32[]{:S(2)}) async-start(bf16[6,192,256]{2,1,0:T(8,128)(2,1)} %broadcast_in_dim.6), calls=%async_computation | async-start | bytes 1179648 | tf_op jit(solution)/shard_map/all_to_all | solution.py:32
  15.0 0.0 copy-done.1
  15.1 9.7 %collective-permute-start.4 = (bf16[192,256]{1,0:T(8,128)(2,1)S(1)}, bf16[192,256]{1,0:T(8,128)(2,1)S(1)}, u32[]{:S(2)}, u32[]{:S(2)}) collective-permute-start(bf16[192,256]{1,0:T(8,128)(2,1)S(1)} %copy-done.1), channel_id=1, source_target_pairs={{0,48},{48,0},{1,49},{49,1},{2,50},{50,2},{3,51},{51,3},{4,52},{52... | collective-permute-start | bytes 294920 | tf_op jit(solution)/shard_map/ppermute | solution.py:21
  24.8 11.5 %collective-permute-done.4 = bf16[192,256]{1,0:T(8,128)(2,1)S(1)} collective-permute-done((bf16[192,256]{1,0:T(8,128)(2,1)S(1)}, bf16[192,256]{1,0:T(8,128)(2,1)S(1)}, u32[]{:S(2)}, u32[]{:S(2)}) %collective-permute-start.4) | collective-permute-done | bytes 98336 | tf_op jit(solution)/shard_map/ppermute | solution.py:21
  36.4 4.6 %collective-permute-start.5 = (bf16[2,192,256]{2,1,0:T(8,128)(2,1)S(1)}, bf16[2,192,256]{2,1,0:T(8,128)(2,1)S(1)}, u32[]{:S(2)}, u32[]{:S(2)}) collective-permute-start(bf16[2,192,256]{2,1,0:T(8,128)(2,1)S(1)} %maximum_select_fusion.2), channel_id=1, source_target_pairs={{0,24},{24,0},{1,25},{25,1},{2,26},{26,2},{3,27},{27,3},{4,28},{28... | collective-permute-start | bytes 589832 | tf_op jit(solution)/shard_map/ppermute | solution.py:21
  41.0 1.0 collective-permute-done.5
  42.1 5.9 %collective-permute-start.7 = (bf16[768,256]{1,0:T(8,128)(2,1)S(1)}, bf16[768,256]{1,0:T(8,128)(2,1)S(1)}, u32[]{:S(2)}, u32[]{:S(2)}) collective-permute-start(bf16[768,256]{1,0:T(8,128)(2,1)S(1)} %bitcast.21), channel_id=1, source_target_pairs={{0,192},{24,600},{96,288},{120,696},{192,384},{216,24},{288,480},{... | collective-permute-start | bytes 1179656 | tf_op jit(solution)/shard_map/ppermute | solution.py:28
  48.0 0.0 all-to-all-done
  48.0 3.1 %collective-permute-start = (bf16[2,3,192,256]{3,2,1,0:T(8,128)(2,1)S(1)}, bf16[2,3,192,256]{3,2,1,0:T(8,128)(2,1)S(1)}, u32[]{:S(2)}, u32[]{:S(2)}) collective-permute-start(bf16[2,3,192,256]{3,2,1,0:T(8,128)(2,1)S(1)} %bitcast.18), channel_id=1, source_target_pairs={{0,6},{6,12},{12,18},{18,0},{1,7},{7,13},{13,19},{19,1},{2,8},{8,1... | collective-permute-start | bytes 1769480 | tf_op jit(solution)/shard_map/ppermute | solution.py:21
  51.1 3.0 %collective-permute-start.6 = (bf16[768,256]{1,0:T(8,128)(2,1)S(1)}, bf16[768,256]{1,0:T(8,128)(2,1)S(1)}, u32[]{:S(2)}, u32[]{:S(2)}) collective-permute-start(bf16[768,256]{1,0:T(8,128)(2,1)S(1)} %bitcast.22), channel_id=1, source_target_pairs={{0,96},{24,696},{96,192},{120,24},{192,288},{216,120},{288,384},{3... | collective-permute-start | bytes 1179656 | tf_op jit(solution)/shard_map/ppermute | solution.py:28
  54.1 2.8 %collective-permute-done.7.refs_7_ = bf16[768,256]{1,0:T(8,128)(2,1)S(1)} collective-permute-done((bf16[768,256]{1,0:T(8,128)(2,1)S(1)}, bf16[768,256]{1,0:T(8,128)(2,1)S(1)}, u32[]{:S(2)}, u32[]{:S(2)}) %collective-permute-start.7) | collective-permute-done | bytes 393248 | tf_op jit(solution)/shard_map/ppermute | solution.py:28
  56.9 4.2 %collective-permute-start.8 = (bf16[768,256]{1,0:T(8,128)(2,1)S(1)}, bf16[768,256]{1,0:T(8,128)(2,1)S(1)}, u32[]{:S(2)}, u32[]{:S(2)}) collective-permute-start(bf16[768,256]{1,0:T(8,128)(2,1)S(1)} %collective-permute-done.7.refs_7_), channel_id=1, source_target_pairs={{0,96},{24,696},{96,192},{120,24},{192,288},{216,120},{288,384},{3... | collective-permute-start | bytes 1179656 | tf_op jit(solution)/shard_map/ppermute | solution.py:28
  61.1 4.4 %collective-permute-start.1 = (bf16[2,3,192,256]{3,2,1,0:T(8,128)(2,1)S(1)}, bf16[2,3,192,256]{3,2,1,0:T(8,128)(2,1)S(1)}, u32[]{:S(2)}, u32[]{:S(2)}) collective-permute-start(bf16[2,3,192,256]{3,2,1,0:T(8,128)(2,1)S(1)} %bitcast.19), channel_id=1, source_target_pairs={{0,18},{6,0},{12,6},{18,12},{1,19},{7,1},{13,7},{19,13},{2,20},{8,... | collective-permute-start | bytes 1769480 | tf_op jit(solution)/shard_map/ppermute | solution.py:21
  65.5 3.7 %collective-permute-start.9 = (bf16[384,256]{1,0:T(8,128)(2,1)S(1)}, bf16[384,256]{1,0:T(8,128)(2,1)S(1)}, u32[]{:S(2)}, u32[]{:S(2)}) collective-permute-start(bf16[384,256]{1,0:T(8,128)(2,1)S(1)} %constant_dynamic-slice_fusion.4), channel_id=1, source_target_pairs={{0,192},{24,600},{96,288},{120,696},{192,384},{216,24},{288,480},{... | collective-permute-start | bytes 589832 | tf_op jit(solution)/shard_map/ppermute | solution.py:28
  69.3 0.0 collective-permute-done.6.refs_6_
  69.3 2.6 %collective-permute-start.11 = (bf16[768,256]{1,0:T(8,128)(2,1)S(1)}, bf16[768,256]{1,0:T(8,128)(2,1)S(1)}, u32[]{:S(2)}, u32[]{:S(2)}) collective-permute-start(bf16[768,256]{1,0:T(8,128)(2,1)S(1)} %collective-permute-done.7.refs_7_), channel_id=1, source_target_pairs={{0,24},{24,0},{1,25},{25,1},{2,26},{26,2},{3,27},{27,3},{4,28},{28... | collective-permute-start | bytes 1179656 | tf_op jit(solution)/shard_map/ppermute | solution.py:21
  71.9 2.3 %collective-permute-done.9.refs_9_ = bf16[384,256]{1,0:T(8,128)(2,1)S(1)} collective-permute-done((bf16[384,256]{1,0:T(8,128)(2,1)S(1)}, bf16[384,256]{1,0:T(8,128)(2,1)S(1)}, u32[]{:S(2)}, u32[]{:S(2)}) %collective-permute-start.9) | collective-permute-done | bytes 196640 | tf_op jit(solution)/shard_map/ppermute | solution.py:28
  74.2 4.7 %collective-permute-start.10 = (bf16[768,256]{1,0:T(8,128)(2,1)S(1)}, bf16[768,256]{1,0:T(8,128)(2,1)S(1)}, u32[]{:S(2)}, u32[]{:S(2)}) collective-permute-start(bf16[768,256]{1,0:T(8,128)(2,1)S(1)} %collective-permute-done.6.refs_6_), channel_id=1, source_target_pairs={{0,24},{24,0},{1,25},{25,1},{2,26},{26,2},{3,27},{27,3},{4,28},{28... | collective-permute-start | bytes 1179656 | tf_op jit(solution)/shard_map/ppermute | solution.py:21
  78.9 0.0 collective-permute-done.8.refs_8_
  78.9 1.9 %collective-permute-start.13 = (bf16[384,256]{1,0:T(8,128)(2,1)S(1)}, bf16[384,256]{1,0:T(8,128)(2,1)S(1)}, u32[]{:S(2)}, u32[]{:S(2)}) collective-permute-start(bf16[384,256]{1,0:T(8,128)(2,1)S(1)} %collective-permute-done.9.refs_9_), channel_id=1, source_target_pairs={{0,24},{24,0},{1,25},{25,1},{2,26},{26,2},{3,27},{27,3},{4,28},{28... | collective-permute-start | bytes 589832 | tf_op jit(solution)/shard_map/ppermute | solution.py:21
  80.8 0.0 collective-permute-done.refs_1_
  80.8 2.4 %collective-permute-start.12 = (bf16[768,256]{1,0:T(8,128)(2,1)S(1)}, bf16[768,256]{1,0:T(8,128)(2,1)S(1)}, u32[]{:S(2)}, u32[]{:S(2)}) collective-permute-start(bf16[768,256]{1,0:T(8,128)(2,1)S(1)} %collective-permute-done.8.refs_8_), channel_id=1, source_target_pairs={{0,24},{24,0},{1,25},{25,1},{2,26},{26,2},{3,27},{27,3},{4,28},{28... | collective-permute-start | bytes 1179656 | tf_op jit(solution)/shard_map/ppermute | solution.py:21
  83.3 0.0 collective-permute-done.1.refs_2_
  83.3 1.9 %collective-permute-start.2 = (bf16[3,192,256]{2,1,0:T(8,128)(2,1)S(1)}, bf16[3,192,256]{2,1,0:T(8,128)(2,1)S(1)}, u32[]{:S(2)}, u32[]{:S(2)}) collective-permute-start(bf16[3,192,256]{2,1,0:T(8,128)(2,1)S(1)} %slice_bitcast_fusion.1), channel_id=1, source_target_pairs={{0,6},{6,12},{12,18},{18,0},{1,7},{7,13},{13,19},{19,1},{2,8},{8,1... | collective-permute-start | bytes 884744 | tf_op jit(solution)/shard_map/ppermute | solution.py:21
  85.3 0.0 collective-permute-done.13.refs_13_
  85.3 4.6 %collective-permute-start.3 = (bf16[3,192,256]{2,1,0:T(8,128)(2,1)S(1)}, bf16[3,192,256]{2,1,0:T(8,128)(2,1)S(1)}, u32[]{:S(2)}, u32[]{:S(2)}) collective-permute-start(bf16[3,192,256]{2,1,0:T(8,128)(2,1)S(1)} %slice_bitcast_fusion), channel_id=1, source_target_pairs={{0,18},{6,0},{12,6},{18,12},{1,19},{7,1},{13,7},{19,13},{2,20},{8,... | collective-permute-start | bytes 884744 | tf_op jit(solution)/shard_map/ppermute | solution.py:21
  89.9 0.0 collective-permute-done.11.refs_11_
  89.9 0.0 collective-permute-done.10.refs_10_
  89.9 0.0 collective-permute-done.12.refs_12_
  89.9 5.1 %collective-permute-done.2.refs_3_ = bf16[3,192,256]{2,1,0:T(8,128)(2,1)S(1)} collective-permute-done((bf16[3,192,256]{2,1,0:T(8,128)(2,1)S(1)}, bf16[3,192,256]{2,1,0:T(8,128)(2,1)S(1)}, u32[]{:S(2)}, u32[]{:S(2)}) %collective-permute-start.2) | collective-permute-done | bytes 294944 | tf_op jit(solution)/shard_map/ppermute | solution.py:21
  95.0 0.9 collective-permute-done.3.refs_4_
  95.9 2.0 %first.1 = (f32[192,256]{1,0:T(8,128)}, bf16[8,2,2,8,192]{4,3,2,1,0:T(8,128)(2,1)S(1)}) custom-call(bf16[2,3,192,256]{3,2,1,0:T(8,128)(2,1)S(1)} %bitcast.20, bf16[2,3,192,256]{3,2,1,0:T(8,128)(2,1)S(1)} %collective-permute-done.refs_1_, bf16[2,3,192,256]{3,2,1,0:T(8,128)(2,1)S(1)} %collective-permute-done.1.refs_2_, ...), custom_call_target="tpu_custom_call" | custom-call | tf_op jit(solution)/shard_map/first/pallas_call | solution.py:107
  97.9 0.0 copy-start
  97.9 17.0 %all_to_all.20 = bf16[16,2,8,192]{3,2,1,0:T(8,128)(2,1)S(1)} all-to-all(bf16[16,2,8,192]{3,2,1,0:T(8,128)(2,1)S(1)} %bitcast.24), channel_id=1, replica_groups=mesh['y'=8,'zh'=2,'co'=2,'x'=4,'zl'=6] {'y','co'}, dimensions={0} | all-to-all | bytes 196608 | tf_op jit(solution)/shard_map/all_to_all | solution.py:32
  115.0 0.1 copy.5
  115.0 0.1 broadcast_in_dim.14
  115.2 0.9 broadcast_in_dim.15
  116.0 19.9 %all-to-all-start.2 = ((bf16[48,8,768]{2,1,0:T(8,128)(2,1)}), bf16[48,8,768]{2,1,0:T(8,128)(2,1)S(1)}, u32[]{:S(2)}, u32[]{:S(2)}) async-start(bf16[48,8,768]{2,1,0:T(8,128)(2,1)} %bitcast.12), calls=%async_computation.2 | async-start | bytes 1179648 | tf_op jit(solution)/shard_map/all_to_all | solution.py:32
  136.0 0.0 copy-done
  136.0 0.1 constant_dynamic-slice_fusion
  136.1 3.0 %collective-permute-start.14 = (bf16[1536,128]{1,0:T(8,128)(2,1)S(1)}, bf16[1536,128]{1,0:T(8,128)(2,1)S(1)}, u32[]{:S(2)}, u32[]{:S(2)}) collective-permute-start(bf16[1536,128]{1,0:T(8,128)(2,1)S(1)} %get-tuple-element.7), channel_id=1, source_target_pairs={{0,6},{6,12},{12,18},{18,0},{1,7},{7,13},{13,19},{19,1},{2,8},{8,1... | collective-permute-start | bytes 1179656 | tf_op jit(solution)/shard_map/ppermute | solution.py:21
  139.2 4.3 %collective-permute-start.15 = (bf16[1536,128]{1,0:T(8,128)(2,1)S(1)}, bf16[1536,128]{1,0:T(8,128)(2,1)S(1)}, u32[]{:S(2)}, u32[]{:S(2)}) collective-permute-start(bf16[1536,128]{1,0:T(8,128)(2,1)S(1)} %get-tuple-element.9), channel_id=1, source_target_pairs={{0,12},{6,18},{12,0},{18,6},{1,13},{7,19},{13,1},{19,7},{2,14},{8,... | collective-permute-start | bytes 1179656 | tf_op jit(solution)/shard_map/ppermute | solution.py:21
  143.5 3.1 %collective-permute-start.16 = (bf16[1536,128]{1,0:T(8,128)(2,1)S(1)}, bf16[1536,128]{1,0:T(8,128)(2,1)S(1)}, u32[]{:S(2)}, u32[]{:S(2)}) collective-permute-start(bf16[1536,128]{1,0:T(8,128)(2,1)S(1)} %get-tuple-element.6), channel_id=1, source_target_pairs={{0,18},{6,0},{12,6},{18,12},{1,19},{7,1},{13,7},{19,13},{2,20},{8,... | collective-permute-start | bytes 1179656 | tf_op jit(solution)/shard_map/ppermute | solution.py:21
  146.6 6.9 %collective-permute-done.14.refs_1_ = bf16[1536,128]{1,0:T(8,128)(2,1)S(1)} collective-permute-done((bf16[1536,128]{1,0:T(8,128)(2,1)S(1)}, bf16[1536,128]{1,0:T(8,128)(2,1)S(1)}, u32[]{:S(2)}, u32[]{:S(2)}) %collective-permute-start.14) | collective-permute-done | bytes 393248 | tf_op jit(solution)/shard_map/ppermute | solution.py:21
  153.5 11.2 %collective-permute-done.15.refs_2_ = bf16[1536,128]{1,0:T(8,128)(2,1)S(1)} collective-permute-done((bf16[1536,128]{1,0:T(8,128)(2,1)S(1)}, bf16[1536,128]{1,0:T(8,128)(2,1)S(1)}, u32[]{:S(2)}, u32[]{:S(2)}) %collective-permute-start.15) | collective-permute-done | bytes 393248 | tf_op jit(solution)/shard_map/ppermute | solution.py:21
  164.6 0.4 collective-permute-done.16.refs_3_
  165.1 0.0 all-to-all-done.2
  165.1 0.8 second.1
  165.8 11.1 %all_to_all.21 = f32[4,192,128]{2,1,0:T(8,128)S(1)} all-to-all(f32[4,192,128]{2,1,0:T(8,128)S(1)} %second.1), channel_id=1, replica_groups=mesh['y'=8,'zh'=2,'co'=2,'x'=4,'zl'=6] {'x'}, dimensions={0} | all-to-all | bytes 786432 | tf_op jit(solution)/shard_map/all_to_all | solution.py:32
  177.0 0.7 reduce_sum.9
  (6 shorter events, 0.1 us)
Async XLA Ops:
  0.6 14.4 %copy-start.1 = (bf16[192,256]{1,0:T(8,128)(2,1)S(1)}, bf16[192,256]{1,0:T(8,128)(2,1)}, u32[]{:S(2)}) copy-start(bf16[192,256]{1,0:T(8,128)(2,1)} %param.4) | copy-start | bytes 294916
  2.4 45.6 %all-to-all-start = ((bf16[6,192,256]{2,1,0:T(8,128)(2,1)}), bf16[6,192,256]{2,1,0:T(8,128)(2,1)S(1)}, u32[]{:S(2)}, u32[]{:S(2)}) async-start(bf16[6,192,256]{2,1,0:T(8,128)(2,1)} %broadcast_in_dim.6), calls=%async_computation | async-start | bytes 1179648 | tf_op jit(solution)/shard_map/all_to_all | solution.py:32
  15.1 21.3 %collective-permute-start.4 = (bf16[192,256]{1,0:T(8,128)(2,1)S(1)}, bf16[192,256]{1,0:T(8,128)(2,1)S(1)}, u32[]{:S(2)}, u32[]{:S(2)}) collective-permute-start(bf16[192,256]{1,0:T(8,128)(2,1)S(1)} %copy-done.1), channel_id=1, source_target_pairs={{0,48},{48,0},{1,49},{49,1},{2,50},{50,2},{3,51},{51,3},{4,52},{52... | collective-permute-start | bytes 294920 | tf_op jit(solution)/shard_map/ppermute | solution.py:21
  36.4 5.7 %collective-permute-start.5 = (bf16[2,192,256]{2,1,0:T(8,128)(2,1)S(1)}, bf16[2,192,256]{2,1,0:T(8,128)(2,1)S(1)}, u32[]{:S(2)}, u32[]{:S(2)}) collective-permute-start(bf16[2,192,256]{2,1,0:T(8,128)(2,1)S(1)} %maximum_select_fusion.2), channel_id=1, source_target_pairs={{0,24},{24,0},{1,25},{25,1},{2,26},{26,2},{3,27},{27,3},{4,28},{28... | collective-permute-start | bytes 589832 | tf_op jit(solution)/shard_map/ppermute | solution.py:21
  42.1 14.8 %collective-permute-start.7 = (bf16[768,256]{1,0:T(8,128)(2,1)S(1)}, bf16[768,256]{1,0:T(8,128)(2,1)S(1)}, u32[]{:S(2)}, u32[]{:S(2)}) collective-permute-start(bf16[768,256]{1,0:T(8,128)(2,1)S(1)} %bitcast.21), channel_id=1, source_target_pairs={{0,192},{24,600},{96,288},{120,696},{192,384},{216,24},{288,480},{... | collective-permute-start | bytes 1179656 | tf_op jit(solution)/shard_map/ppermute | solution.py:28
  48.0 32.8 %collective-permute-start = (bf16[2,3,192,256]{3,2,1,0:T(8,128)(2,1)S(1)}, bf16[2,3,192,256]{3,2,1,0:T(8,128)(2,1)S(1)}, u32[]{:S(2)}, u32[]{:S(2)}) collective-permute-start(bf16[2,3,192,256]{3,2,1,0:T(8,128)(2,1)S(1)} %bitcast.18), channel_id=1, source_target_pairs={{0,6},{6,12},{12,18},{18,0},{1,7},{7,13},{13,19},{19,1},{2,8},{8,1... | collective-permute-start | bytes 1769480 | tf_op jit(solution)/shard_map/ppermute | solution.py:21
  51.1 18.2 %collective-permute-start.6 = (bf16[768,256]{1,0:T(8,128)(2,1)S(1)}, bf16[768,256]{1,0:T(8,128)(2,1)S(1)}, u32[]{:S(2)}, u32[]{:S(2)}) collective-permute-start(bf16[768,256]{1,0:T(8,128)(2,1)S(1)} %bitcast.22), channel_id=1, source_target_pairs={{0,96},{24,696},{96,192},{120,24},{192,288},{216,120},{288,384},{3... | collective-permute-start | bytes 1179656 | tf_op jit(solution)/shard_map/ppermute | solution.py:28
  56.9 22.0 %collective-permute-start.8 = (bf16[768,256]{1,0:T(8,128)(2,1)S(1)}, bf16[768,256]{1,0:T(8,128)(2,1)S(1)}, u32[]{:S(2)}, u32[]{:S(2)}) collective-permute-start(bf16[768,256]{1,0:T(8,128)(2,1)S(1)} %collective-permute-done.7.refs_7_), channel_id=1, source_target_pairs={{0,96},{24,696},{96,192},{120,24},{192,288},{216,120},{288,384},{3... | collective-permute-start | bytes 1179656 | tf_op jit(solution)/shard_map/ppermute | solution.py:28
  61.1 22.2 %collective-permute-start.1 = (bf16[2,3,192,256]{3,2,1,0:T(8,128)(2,1)S(1)}, bf16[2,3,192,256]{3,2,1,0:T(8,128)(2,1)S(1)}, u32[]{:S(2)}, u32[]{:S(2)}) collective-permute-start(bf16[2,3,192,256]{3,2,1,0:T(8,128)(2,1)S(1)} %bitcast.19), channel_id=1, source_target_pairs={{0,18},{6,0},{12,6},{18,12},{1,19},{7,1},{13,7},{19,13},{2,20},{8,... | collective-permute-start | bytes 1769480 | tf_op jit(solution)/shard_map/ppermute | solution.py:21
  65.5 8.6 %collective-permute-start.9 = (bf16[384,256]{1,0:T(8,128)(2,1)S(1)}, bf16[384,256]{1,0:T(8,128)(2,1)S(1)}, u32[]{:S(2)}, u32[]{:S(2)}) collective-permute-start(bf16[384,256]{1,0:T(8,128)(2,1)S(1)} %constant_dynamic-slice_fusion.4), channel_id=1, source_target_pairs={{0,192},{24,600},{96,288},{120,696},{192,384},{216,24},{288,480},{... | collective-permute-start | bytes 589832 | tf_op jit(solution)/shard_map/ppermute | solution.py:28
  69.3 20.6 %collective-permute-start.11 = (bf16[768,256]{1,0:T(8,128)(2,1)S(1)}, bf16[768,256]{1,0:T(8,128)(2,1)S(1)}, u32[]{:S(2)}, u32[]{:S(2)}) collective-permute-start(bf16[768,256]{1,0:T(8,128)(2,1)S(1)} %collective-permute-done.7.refs_7_), channel_id=1, source_target_pairs={{0,24},{24,0},{1,25},{25,1},{2,26},{26,2},{3,27},{27,3},{4,28},{28... | collective-permute-start | bytes 1179656 | tf_op jit(solution)/shard_map/ppermute | solution.py:21
  74.2 15.7 %collective-permute-start.10 = (bf16[768,256]{1,0:T(8,128)(2,1)S(1)}, bf16[768,256]{1,0:T(8,128)(2,1)S(1)}, u32[]{:S(2)}, u32[]{:S(2)}) collective-permute-start(bf16[768,256]{1,0:T(8,128)(2,1)S(1)} %collective-permute-done.6.refs_6_), channel_id=1, source_target_pairs={{0,24},{24,0},{1,25},{25,1},{2,26},{26,2},{3,27},{27,3},{4,28},{28... | collective-permute-start | bytes 1179656 | tf_op jit(solution)/shard_map/ppermute | solution.py:21
  78.9 6.4 %collective-permute-start.13 = (bf16[384,256]{1,0:T(8,128)(2,1)S(1)}, bf16[384,256]{1,0:T(8,128)(2,1)S(1)}, u32[]{:S(2)}, u32[]{:S(2)}) collective-permute-start(bf16[384,256]{1,0:T(8,128)(2,1)S(1)} %collective-permute-done.9.refs_9_), channel_id=1, source_target_pairs={{0,24},{24,0},{1,25},{25,1},{2,26},{26,2},{3,27},{27,3},{4,28},{28... | collective-permute-start | bytes 589832 | tf_op jit(solution)/shard_map/ppermute | solution.py:21
  80.8 9.0 %collective-permute-start.12 = (bf16[768,256]{1,0:T(8,128)(2,1)S(1)}, bf16[768,256]{1,0:T(8,128)(2,1)S(1)}, u32[]{:S(2)}, u32[]{:S(2)}) collective-permute-start(bf16[768,256]{1,0:T(8,128)(2,1)S(1)} %collective-permute-done.8.refs_8_), channel_id=1, source_target_pairs={{0,24},{24,0},{1,25},{25,1},{2,26},{26,2},{3,27},{27,3},{4,28},{28... | collective-permute-start | bytes 1179656 | tf_op jit(solution)/shard_map/ppermute | solution.py:21
  83.3 11.7 %collective-permute-start.2 = (bf16[3,192,256]{2,1,0:T(8,128)(2,1)S(1)}, bf16[3,192,256]{2,1,0:T(8,128)(2,1)S(1)}, u32[]{:S(2)}, u32[]{:S(2)}) collective-permute-start(bf16[3,192,256]{2,1,0:T(8,128)(2,1)S(1)} %slice_bitcast_fusion.1), channel_id=1, source_target_pairs={{0,6},{6,12},{12,18},{18,0},{1,7},{7,13},{13,19},{19,1},{2,8},{8,1... | collective-permute-start | bytes 884744 | tf_op jit(solution)/shard_map/ppermute | solution.py:21
  85.3 10.6 %collective-permute-start.3 = (bf16[3,192,256]{2,1,0:T(8,128)(2,1)S(1)}, bf16[3,192,256]{2,1,0:T(8,128)(2,1)S(1)}, u32[]{:S(2)}, u32[]{:S(2)}) collective-permute-start(bf16[3,192,256]{2,1,0:T(8,128)(2,1)S(1)} %slice_bitcast_fusion), channel_id=1, source_target_pairs={{0,18},{6,0},{12,6},{18,12},{1,19},{7,1},{13,7},{19,13},{2,20},{8,... | collective-permute-start | bytes 884744 | tf_op jit(solution)/shard_map/ppermute | solution.py:21
  97.9 38.1 %copy-start = (bf16[6144,128]{1,0:T(8,128)(2,1)S(1)}, bf16[6144,128]{1,0:T(8,128)(2,1)}, u32[]{:S(2)}) copy-start(bf16[6144,128]{1,0:T(8,128)(2,1)} %param.5) | copy-start | bytes 4718596
  116.0 49.0 %all-to-all-start.2 = ((bf16[48,8,768]{2,1,0:T(8,128)(2,1)}), bf16[48,8,768]{2,1,0:T(8,128)(2,1)S(1)}, u32[]{:S(2)}, u32[]{:S(2)}) async-start(bf16[48,8,768]{2,1,0:T(8,128)(2,1)} %bitcast.12), calls=%async_computation.2 | async-start | bytes 1179648 | tf_op jit(solution)/shard_map/all_to_all | solution.py:32
  136.1 17.4 %collective-permute-start.14 = (bf16[1536,128]{1,0:T(8,128)(2,1)S(1)}, bf16[1536,128]{1,0:T(8,128)(2,1)S(1)}, u32[]{:S(2)}, u32[]{:S(2)}) collective-permute-start(bf16[1536,128]{1,0:T(8,128)(2,1)S(1)} %get-tuple-element.7), channel_id=1, source_target_pairs={{0,6},{6,12},{12,18},{18,0},{1,7},{7,13},{13,19},{19,1},{2,8},{8,1... | collective-permute-start | bytes 1179656 | tf_op jit(solution)/shard_map/ppermute | solution.py:21
  139.2 25.5 %collective-permute-start.15 = (bf16[1536,128]{1,0:T(8,128)(2,1)S(1)}, bf16[1536,128]{1,0:T(8,128)(2,1)S(1)}, u32[]{:S(2)}, u32[]{:S(2)}) collective-permute-start(bf16[1536,128]{1,0:T(8,128)(2,1)S(1)} %get-tuple-element.9), channel_id=1, source_target_pairs={{0,12},{6,18},{12,0},{18,6},{1,13},{7,19},{13,1},{19,7},{2,14},{8,... | collective-permute-start | bytes 1179656 | tf_op jit(solution)/shard_map/ppermute | solution.py:21
  143.5 21.6 %collective-permute-start.16 = (bf16[1536,128]{1,0:T(8,128)(2,1)S(1)}, bf16[1536,128]{1,0:T(8,128)(2,1)S(1)}, u32[]{:S(2)}, u32[]{:S(2)}) collective-permute-start(bf16[1536,128]{1,0:T(8,128)(2,1)S(1)} %get-tuple-element.6), channel_id=1, source_target_pairs={{0,18},{6,0},{12,6},{18,12},{1,19},{7,1},{13,7},{19,13},{2,20},{8,... | collective-permute-start | bytes 1179656 | tf_op jit(solution)/shard_map/ppermute | solution.py:21
